TPU v7x, 256 devices: a whole 4x4x8 slice. The times are simulated.
256 devices in a mesh: region: 8 (over x, core), sub: 32 (over y, z).
Axes of the slice: x: 4, y: 4, z: 8, core: 2. Of those that a mesh axis runs over, the one named last changes fastest.
Arguments:
- multipliers: float32 [256, 3, 3, 256], P(('region', 'sub')), may hold values from -6 to 6
- direction: float32 [256, 3, 3, 256], P(('region', 'sub')), may hold values from -12 to 12
- residual: float32 [256, 3, 3, 256], P(('region', 'sub')), may hold values from -12 to 12
- reaction: float32 [256, 16, 256], P(('region', 'sub')), may hold values from 0.1 to 2
- viscosity: float32 [256, 16, 256], P(('region', 'sub')), may hold values from 0.5 to 5
- primal_index: int32 [256, 96], P(('region', 'sub')), may hold values from 17 to 2286, as said below
- region_inverse: float32 [8, 3072, 3072], P('region', 'sub'), as said below
- coarse_map: float32 [256, 96, 384], P(('region', 'sub')), may hold values from -0.4375 to 0.4375
- global_inverse: float32 [384, 384], replicated, as said below
Outputs:
- new_multipliers: float32 [256, 3, 3, 256], P(('region', 'sub'))
- new_residual: float32 [256, 3, 3, 256], P(('region', 'sub'))
- velocity: float32 [256, 3, 16, 256], P(('region', 'sub'))
- pressure: float32 [256, 16, 256], P(('region', 'sub'))
Inputs may be any that keep to these rules, and one draw needn't show every extreme that they name: `primal_index`: each row holds 96 different positions, each in the interior of a face (neither face index 0 nor 16 - 1); every row contains the first such position and the last one. `region_inverse`: each region's matrix is symmetric positive definite. `global_inverse`: symmetric positive definite.
All inputs are finite; a program needn't handle non-finite values.
Results may differ from a plain program's by a relative error of at most 0.0001.
Values sent between devices are 32-bit elements; how exact they have to be, the bound alone decides.
A program may use at most 64 MiB of HBM per device.

v0:
```python
import jax
import jax.numpy as jnp
from jax import lax
from jax.sharding import PartitionSpec as P

DOM_Z = 4
LEVELS = 3
SWEEPS = 1
COARSE_SWEEPS = 8
VCYCLES = 2


damping = 0.8


def shifted_2(x, axis, by):
    count = lax.axis_size(axis)
    return lax.ppermute(x, axis, [(i, (i + by) % count) for i in range(count)])


def operate(field, react, weight, cells):
    width = field.shape[-1]
    padded = jnp.pad(field, ((0, 0), (1, 1), (cells, cells)))
    middle = padded[:, 1:-1]
    position = lax.broadcasted_iota(jnp.int32, (1, 1, width), 2) % cells
    above = jnp.where(position < cells - 1, middle[:, :, cells + 1 : cells + 1 + width], 0.0)
    beneath = jnp.where(position > 0, middle[:, :, cells - 1 : cells - 1 + width], 0.0)
    beside = padded[:, 2:, cells : cells + width] + padded[:, :-2, cells : cells + width]
    beside = beside + middle[:, :, 2 * cells :] + middle[:, :, :width]
    beside = beside + above + beneath
    return react * field + weight * (6.0 * field - beside)


def restrict(array, cells):
    lead = array.shape[:-2]
    depth = array.shape[-2]
    half = cells // 2
    blocks = array.reshape(lead + (depth // 2, 2, half, 2, half, 2)).mean(axis=(-5, -3, -1))
    return blocks.reshape(lead + (depth // 2, half * half))


def prolong(array, cells):
    lead = array.shape[:-2]
    depth = array.shape[-2]
    cubic = array.reshape(lead + (depth, cells, cells))
    grown = jnp.repeat(jnp.repeat(jnp.repeat(cubic, 2, axis=-3), 2, axis=-2), 2, axis=-1)
    return grown.reshape(lead + (2 * depth, 4 * cells * cells))


def relax(field, source, react, weight, cells, count):
    diagonal = react + 6.0 * weight
    for _ in range(count):
        field = field + damping * (source - operate(field, react, weight, cells)) / diagonal
    return field


def vcycle(field, source, reacts, cells, level):
    weight = 0.25**level
    if level == LEVELS - 1:
        return relax(field, source, reacts[level], weight, cells, COARSE_SWEEPS)
    field = relax(field, source, reacts[level], weight, cells, SWEEPS)
    remain = restrict(source - operate(field, reacts[level], weight, cells), cells)
    coarse = vcycle(jnp.zeros_like(remain), remain, reacts, cells // 2, level + 1)
    field = field + prolong(coarse, cells // 2)
    return relax(field, source, reacts[level], weight, cells, SWEEPS)


def local_solve(source, react, cells):
    reacts = [react]
    size_now = cells
    for _ in range(LEVELS - 1):
        reacts.append(restrict(reacts[-1], size_now))
        size_now = size_now // 2
    field = jnp.zeros_like(source)
    for _ in range(VCYCLES):
        field = vcycle(field, source, reacts, cells, 0)
    return field


def face_cells(picked, cells):
    face = cells * cells
    block = picked // (3 * face)
    component = picked // face % 3
    spot = picked % face
    first = spot // cells
    second = spot % cells
    upper = cells - 1
    place = jnp.where(
        block == 0,
        upper * face + spot,
        jnp.where(
            block == 1, first * face + upper * cells + second, first * face + second * cells + upper
        ),
    )
    return component * (cells * face) + place


def body(
    multipliers,
    direction,
    residual,
    reaction,
    viscosity,
    primal_index,
    region_inverse,
    coarse_map,
    global_inverse,
):
    highest = lax.Precision.HIGHEST
    react = reaction[0]
    cells = react.shape[0]
    face = react.shape[1]
    upper_end = cells - 1
    active = direction[0]
    below_x = shifted_2(active[0], "region", 1)
    below_y = shifted_2(active[1], "sub", DOM_Z)
    below_z = shifted_2(active[2], "sub", 1)
    source = jnp.zeros((3, cells, face), jnp.float32)
    source = source.at[:, upper_end, :].add(active[0])
    source = source.at[:, :, face - cells :].add(active[1].reshape(3, cells, cells))
    source = source.at[:, :, upper_end::cells].add(active[2].reshape(3, cells, cells))
    source = source.at[:, 0, :].add(-below_x)
    source = source.at[:, :, :cells].add(-below_y.reshape(3, cells, cells))
    source = source.at[:, :, 0::cells].add(-below_z.reshape(3, cells, cells))
    picked = primal_index[0]
    primal = jnp.take(active.reshape(-1), picked)
    rows = region_inverse[0]
    mapping = coarse_map[0]
    share = jnp.dot(primal, mapping, precision=highest)
    total = lax.psum(share, ("region", "sub"))
    region_part = jnp.dot(
        rows, lax.all_gather(primal, "sub", axis=0, tiled=True), precision=highest
    )
    top = jnp.dot(global_inverse, total, precision=highest)
    lifted = region_part + jnp.dot(mapping, top, precision=highest)
    base = local_solve(source, react, cells)
    spots = face_cells(picked, cells)
    velocity = base.reshape(-1).at[spots].add(lifted).reshape(3, cells, face)
    upper_x = velocity[:, upper_end, :]
    upper_y = velocity[:, :, face - cells :].reshape(3, face)
    upper_z = velocity[:, :, upper_end::cells].reshape(3, face)
    lower_x = velocity[:, 0, :]
    lower_y = velocity[:, :, :cells].reshape(3, face)
    lower_z = velocity[:, :, 0::cells].reshape(3, face)
    squares = jnp.sum(residual[0] * residual[0])
    after_x = shifted_2(lower_x, "region", -1)
    after_y = shifted_2(lower_y, "sub", -DOM_Z)
    after_z = shifted_2(lower_z, "sub", -1)
    jump = jnp.stack([upper_x - after_x, upper_y - after_y, upper_z - after_z])
    curvature, squares_all = lax.psum((jnp.sum(active * jump), squares), ("region", "sub"))
    step_x = jnp.concatenate([velocity[0, 1:], after_x[0][None]], axis=0) - velocity[0]
    step_y = (
        jnp.concatenate([velocity[1][:, cells:], after_y[1].reshape(cells, cells)], axis=1)
        - velocity[1]
    )
    position = lax.broadcasted_iota(jnp.int32, (1, face), 1) % cells
    edge_values = jnp.repeat(after_z[2].reshape(cells, cells), cells, axis=1)
    shifted = jnp.pad(velocity[2][:, 1:], ((0, 0), (0, 1)))
    step_z = jnp.where(position == cells - 1, edge_values, shifted) - velocity[2]
    pressure = -viscosity[0] * (step_x + step_y + step_z)
    alpha = squares_all / curvature
    new_multipliers = (multipliers[0] + alpha * active)[None]
    new_residual = (residual[0] - alpha * jump)[None]
    return (new_multipliers, new_residual, velocity[None], pressure[None])


def solution(mesh):
    in_specs = (
        P(("region", "sub"), None, None, None),
        P(("region", "sub"), None, None, None),
        P(("region", "sub"), None, None, None),
        P(("region", "sub"), None, None),
        P(("region", "sub"), None, None),
        P(("region", "sub"), None),
        P("region", "sub", None),
        P(("region", "sub"), None, None),
        P(),
    )
    out_specs = (
        P(("region", "sub"), None, None, None),
        P(("region", "sub"), None, None, None),
        P(("region", "sub"), None, None, None),
        P(("region", "sub"), None, None),
    )
    return jax.shard_map(body, mesh=mesh, in_specs=in_specs, out_specs=out_specs, check_vma=False)
```

profile of v0, /device:TPU:1, one launch (start us, length us, event | category | flops | bytes accessed | tf_op | source)
XLA Modules:
  0.0 369.7 jit_solution(10086883032054162801)
XLA Ops:
  0.6 0.8 fusion.286
  1.5 2.6 collective-permute-start
  4.1 6.9 %collective-permute-start.1 = (f32[3,256]{1,0:T(4,128)S(1)}, f32[3,256]{1,0:T(4,128)S(1)}, u32[]{:S(2)}, u32[]{:S(2)}) collective-permute-start(f32[3,256]{1,0:T(4,128)S(1)} %bitcast.181), channel_id=1, source_target_pairs={{0,4},{1,5},{2,6},{3,7},{4,8},{5,9},{6,10},{7,11},{8,12},{9,13},{1... | collective-permute-start | bytes 9224 | tf_op jit(solution)/shard_map/ppermute | solution.py:18
  11.0 0.7 collective-permute-start.2
  11.8 0.7 add_bitcast_fusion
  12.5 0.7 broadcast_multiply_fusion.6
  13.2 1.7 reshape_squeeze.17
  15.4 0.3 copy.126
  15.7 0.3 scatter-add.34
  16.5 1.1 gather_fusion
  17.7 0.6 dynamic-slice.29
  19.1 114.8 %all-reduce.28 = f32[3072]{0:T(1024)S(1)} all-reduce(f32[3072]{0:T(1024)S(1)} %fusion.269), channel_id=1, replica_groups=mesh['region'=8,'sub'=32] {'sub'}, use_global_device_ids=true, to_apply=%add.28 | all-reduce | flops 3072 | bytes 24576
  133.8 0.2 convolution_reduce_fusion
  134.0 100.0 %psum.22 = f32[384]{0:T(512)S(1)} all-reduce(f32[384]{0:T(512)S(1)} %convolution_reduce_fusion), channel_id=1, replica_groups=mesh['region'=8,'sub'=32] {'region','sub'}, use_global_device_ids=true, to_apply=%region_10.11 | all-reduce | flops 384 | bytes 3072 | tf_op jit(solution)/shard_map/psum | solution.py:130
  234.1 0.6 multiply_reduce_fusion
  234.7 1.0 fusion.2
  235.7 0.6 convolution_bitcast_fusion
  236.3 0.3 fusion.5
  237.5 1.1 scatter_fusion
  238.6 0.3 copy.129
  239.4 4.3 %scatter-add.44 = f32[3,16,256]{1,0,2:T(4,128)S(1)} dynamic-update-slice(f32[3,16,256]{1,0,2:T(4,128)S(1)} %scatter_fusion, f32[3,1,256]{1,0,2:T(4,128)S(1)} %slice_add_fusion, s32[]{:T(128)} %constant.334.clone.1, s32[]{:T(128)} %constant.334.clone.1, s32[]{:T(128)} %constant.334.clone.1) | dynamic-update-slice | bytes 6148 | tf_op jit(solution)/shard_map/scatter-add | solution.py:122
  243.7 1.1 scatter_fusion.1
  244.8 2.0 fusion.17
  246.9 2.0 add_subtract_fusion.1
  249.0 4.8 %reshape.713 = f32[3,8,2,8,2,8,2]{6,5,4,3,2,1,0:T(8,128)} reshape(f32[3,16,256]{2,1,0:T(8,128)S(1)} %copy.135) | data formatting | bytes 98304 | tf_op jit(solution)/shard_map/reshape | solution.py:38
  253.8 2.2 reduce_sum.73
  256.6 0.5 reshape.714
  257.1 0.2 reduce_sum.75
  259.1 2.1 bitcast_add_fusion.1
  261.2 2.1 divide_add_fusion.2
  263.3 2.1 divide_add_fusion.1
  265.3 2.2 add_subtract_fusion
  267.7 4.8 %reshape.721 = f32[3,8,2,8,2,8,2]{6,5,4,3,2,1,0:T(8,128)} reshape(f32[3,16,256]{2,1,0:T(8,128)S(1)} %copy.147) | data formatting | bytes 98304 | tf_op jit(solution)/shard_map/reshape | solution.py:38
  272.5 2.2 reduce_sum.77
  275.2 0.5 reshape.722
  275.7 0.2 reduce_sum.78
  277.9 2.1 divide_add_fusion
  280.2 1.1 scatter_fusion.2
  281.4 1.1 collective-permute-start.3
  282.9 0.6 broadcast_in_dim_reshape.2
  283.6 1.3 collective-permute-start.5
  285.0 2.1 collective-permute-start.4
  287.8 3.6 collective-permute-done.4
  291.4 0.6 fusion.100
  292.1 74.3 %all-reduce.29 = (f32[]{:T(128)}, f32[]{:T(128)}) all-reduce(f32[]{:T(128)} %multiply_reduce_fusion, f32[]{:T(128)} %fusion.100), channel_id=1, replica_groups=mesh['region'=8,'sub'=32] {'region','sub'}, use_global_device_ids=true, to_apply=%region_1.0 | all-reduce | flops 2 | bytes 16 | tf_op jit(solution)/shard_map/psum | solution.py:150
  367.8 0.6 copy.163
  368.4 0.6 copy.162
  369.0 0.7 fusion.99
  (162 shorter events, 8.9 us)
Async XLA Ops:
  0.6 234.1 %copy-start = (f32[1,96,3072]{2,1,0:T(8,128)S(1)}, f32[1,96,3072]{2,1,0:T(8,128)}, u32[]{:S(2)}) copy-start(f32[1,96,3072]{2,1,0:T(8,128)} %param.23) | copy-start | bytes 3538948
  1.5 237.1 %collective-permute-start = (f32[3,256]{1,0:T(4,128)S(1)}, f32[3,256]{1,0:T(4,128)S(1)}, u32[]{:S(2)}, u32[]{:S(2)}) collective-permute-start(f32[3,256]{1,0:T(4,128)S(1)} %bitcast.182), channel_id=1, source_target_pairs={{0,32},{32,64},{64,96},{96,128},{128,160},{160,192},{192,224},{224... | collective-permute-start | bytes 9224 | tf_op jit(solution)/shard_map/ppermute | solution.py:18
  4.1 234.8 %collective-permute-start.1 = (f32[3,256]{1,0:T(4,128)S(1)}, f32[3,256]{1,0:T(4,128)S(1)}, u32[]{:S(2)}, u32[]{:S(2)}) collective-permute-start(f32[3,256]{1,0:T(4,128)S(1)} %bitcast.181), channel_id=1, source_target_pairs={{0,4},{1,5},{2,6},{3,7},{4,8},{5,9},{6,10},{7,11},{8,12},{9,13},{1... | collective-permute-start | bytes 9224 | tf_op jit(solution)/shard_map/ppermute | solution.py:18
  11.0 228.0 %collective-permute-start.2 = (f32[3,256]{1,0:T(4,128)S(1)}, f32[3,256]{1,0:T(4,128)S(1)}, u32[]{:S(2)}, u32[]{:S(2)}) collective-permute-start(f32[3,256]{1,0:T(4,128)S(1)} %bitcast.180), channel_id=1, source_target_pairs={{0,1},{1,2},{2,3},{3,4},{4,5},{5,6},{6,7},{7,8},{8,9},{9,10},{10,1... | collective-permute-start | bytes 9224 | tf_op jit(solution)/shard_map/ppermute | solution.py:18
  15.1 1.3 copy-start.8
  15.1 1.3 copy-start.4
  15.4 2.3 copy-start.9
  15.4 118.4 %copy-start.2 = (f32[1,96,384]{2,1,0:T(8,128)S(1)}, f32[1,96,384]{2,1,0:T(8,128)}, u32[]{:S(2)}) copy-start(f32[1,96,384]{2,1,0:T(8,128)} %param.24) | copy-start | bytes 442372
  15.6 218.4 %copy-start.5 = (f32[1,3,3,256]{3,0,2,1:T(1,128)S(1)}, f32[1,3,3,256]{3,0,2,1:T(1,128)}, u32[]{:S(2)}) copy-start(f32[1,3,3,256]{3,0,2,1:T(1,128)} %param.19) | copy-start | bytes 27652
  16.0 219.7 %copy-start.1 = (f32[384,384]{1,0:T(8,128)S(1)}, f32[384,384]{1,0:T(8,128)}, u32[]{:S(2)}) copy-start(f32[384,384]{1,0:T(8,128)} %param.25) | copy-start | bytes 1769476
  234.7 2.4 copy-start.3
  280.2 88.2 %copy-start.7 = (f32[1,3,3,256]{3,0,2,1:T(1,128)S(1)}, f32[1,3,3,256]{3,0,2,1:T(1,128)}, u32[]{:S(2)}) copy-start(f32[1,3,3,256]{3,0,2,1:T(1,128)} %param.17) | copy-start | bytes 27652
  280.2 88.8 %copy-start.6 = (f32[1,16,256]{2,1,0:T(8,128)S(1)}, f32[1,16,256]{2,1,0:T(8,128)}, u32[]{:S(2)}) copy-start(f32[1,16,256]{2,1,0:T(8,128)} %param.21) | copy-start | bytes 49156
  281.4 6.0 %collective-permute-start.3 = (f32[3,256]{1,0:T(4,128)S(1)}, f32[3,256]{1,0:T(4,128)S(1)}, u32[]{:S(2)}, u32[]{:S(2)}) collective-permute-start(f32[3,256]{1,0:T(4,128)S(1)} %bitcast.183), channel_id=1, source_target_pairs={{0,224},{32,0},{64,32},{96,64},{128,96},{160,128},{192,160},{224,1... | collective-permute-start | bytes 9224 | tf_op jit(solution)/shard_map/ppermute | solution.py:18
  283.6 3.8 %collective-permute-start.5 = (f32[3,256]{1,0:T(4,128)S(1)}, f32[3,256]{1,0:T(4,128)S(1)}, u32[]{:S(2)}, u32[]{:S(2)}) collective-permute-start(f32[3,256]{1,0:T(4,128)S(1)} %reshape.734), channel_id=1, source_target_pairs={{0,31},{1,0},{2,1},{3,2},{4,3},{5,4},{6,5},{7,6},{8,7},{9,8},{10,9... | collective-permute-start | bytes 9224 | tf_op jit(solution)/shard_map/ppermute | solution.py:18
  285.0 6.4 %collective-permute-start.4 = (f32[3,256]{1,0:T(4,128)S(1)}, f32[3,256]{1,0:T(4,128)S(1)}, u32[]{:S(2)}, u32[]{:S(2)}) collective-permute-start(f32[3,256]{1,0:T(4,128)S(1)} %reshape.732), channel_id=1, source_target_pairs={{0,28},{1,29},{2,30},{3,31},{4,0},{5,1},{6,2},{7,3},{8,4},{9,5},{1... | collective-permute-start | bytes 9224 | tf_op jit(solution)/shard_map/ppermute | solution.py:18
where the time goes:
time: 371 us; the launch traced here: 370 us
  blocking collectives  289 us (78%)
  other arithmetic  29.4 us (8%)
  local copies, waits for them, and re-layouts  27.2 us (7%)
  starting transfers between devices  14.8 us (4%)
    unnamed x1, blocking collectives  115 us
    psum x1, blocking collectives, body(): total = lax.psum(share, ('region', 'sub'))  100 us
    psum x1, blocking collectives, body(): lax.psum((jnp.sum(active * jump), squares), ('region', 'sub'))  74.3 us
    ppermute x6, starting transfers between devices, shifted_2(): return lax.ppermute(x, axis, [(i, (i + by) % count) for i in range(count)])  14.8 us
    reshape x4, local copies, waits for them, and re-layouts, restrict(): array.reshape(lead + (depth // 2, 2, half, 2, half, 2))  10.7 us
    add x17, other arithmetic, relax(): field + damping * (source - operate(field, react, weight, cells)) / diagonal  7.44 us
  transfers between devices with their start and end apart: 6, of which 1 were waited for; matrix products, arithmetic and copies ran while one was open for 4% of the time, Pallas kernels for 0%

commit v1 on v0

v1 whole, which is shorter than its diff:
```python
import functools

import jax
import jax.numpy as jnp
from jax import lax
from jax.experimental import pallas as pl
from jax.experimental.pallas import tpu as pltpu
from jax.sharding import PartitionSpec as P

DOM_Z = 4
COARSE_SWEEPS = 8
CELLS = 16
FACE = 256
DAMPING = 0.8
KEEP = 0.2
MESH = pl.DeviceIdType.MESH
F32 = jnp.float32
BF16 = jnp.bfloat16


def iota(shape, axis):
    return lax.broadcasted_iota(jnp.int32, shape, axis)


def split(field):
    lead = field.shape[0] // CELLS
    cubic = field.reshape(lead, CELLS, FACE)
    return [cubic[:, 8 * i : 8 * i + 8, 128 * j : 128 * j + 128] for i in (0, 1) for j in (0, 1)]


def join(parts):
    low = jnp.concatenate([parts[0], parts[1]], axis=2)
    high = jnp.concatenate([parts[2], parts[3]], axis=2)
    whole = jnp.concatenate([low, high], axis=1)
    return whole.reshape(whole.shape[0] * CELLS, FACE)


def neighbours(parts, step):
    shape = parts[0].shape
    x = iota(shape, 1)
    lane = iota(shape, 2)
    y = lane >> 4
    z = lane & 15

    def roll(v, by, axis):
        return pltpu.roll(v, by % v.shape[axis], axis)

    sums = []
    ys_up = [roll(v, 16 * step, 2) for v in parts]
    ys_down = ys_up if step == 4 else [roll(v, -16 * step, 2) for v in parts]
    xs_up = [roll(v, step, 1) for v in parts]
    xs_down = xs_up if step == 4 else [roll(v, -step, 1) for v in parts]
    for i in (0, 1):
        for j in (0, 1):
            k = 2 * i + j
            v = parts[k]
            total = jnp.where(z >= step, roll(v, step, 2), 0.0)
            total = total + jnp.where(z < CELLS - step, roll(v, -step, 2), 0.0)
            before = ys_up[k - 1] if j == 1 else 0.0
            total = total + jnp.where(y >= step, ys_up[k], before)
            after = ys_down[k + 1] if j == 0 else 0.0
            total = total + jnp.where(y < 8 - step, ys_down[k], after)
            before = xs_up[k - 2] if i == 1 else 0.0
            total = total + jnp.where(x >= step, xs_up[k], before)
            after = xs_down[k + 2] if i == 0 else 0.0
            total = total + jnp.where(x < 8 - step, xs_down[k], after)
            sums.append(total)
    return sums


def block_mean(parts, step):
    shape = parts[0].shape
    x = iota(shape, 1)
    lane = iota(shape, 2)

    def pair(v, by, axis, even):
        count = v.shape[axis]
        return v + jnp.where(even, pltpu.roll(v, count - by, axis), pltpu.roll(v, by, axis))

    result = []
    for v in parts:
        v = pair(v, step, 2, (lane & step) == 0)
        v = pair(v, 16 * step, 2, ((lane >> 4) & step) == 0)
        v = pair(v, step, 1, (x & step) == 0)
        result.append(v * 0.125)
    return result


def merge(parts):
    spot = iota(parts[0].shape[1:], 1) & 3
    return [jnp.where(spot == 0, v[0], jnp.where(spot == 1, v[1], v[2]))[None] for v in parts]


def unmerge(parts):
    result = []
    for v in parts:
        v = v[0]
        spot = iota(v.shape, 1) & 3
        moved = {by: pltpu.roll(v, by % 128, 1) if by else v for by in range(-2, 4)}
        comps = []
        for c in range(3):
            value = moved[3 - c]
            for t in (2, 1, 0):
                value = jnp.where(spot == t, moved[t - c], value)
            comps.append(value)
        result.append(jnp.stack(comps, axis=0))
    return result


def broad(parts):
    return [jnp.broadcast_to(v, (3,) + v.shape[1:]) for v in parts]


def coarse_solve(source, scale2):
    b = merge(source)
    wb = [w * s for w, s in zip(scale2, b)]
    v = wb
    for _ in range(COARSE_SWEEPS - 1):
        near = neighbours(v, 4)
        v = [KEEP * a + (c + (w * 0.0625) * n) for a, c, w, n in zip(v, wb, scale2, near)]
    return unmerge(v)


def middle_solve(source, scale1, scale2):
    wb = [w * s for w, s in zip(scale1, source)]
    near = neighbours(wb, 2)
    remain = [KEEP * s + 0.25 * n for s, n in zip(source, near)]
    coarse = coarse_solve(block_mean(remain, 2), scale2)
    v = [a + c for a, c in zip(wb, coarse)]
    near = neighbours(v, 2)
    return [KEEP * a + (c + (w * 0.25) * n) for a, c, w, n in zip(v, wb, scale1, near)]


def local_solve(source, diag0, scale0, scale1, scale2):
    wb = [w * s for w, s in zip(scale0, source)]
    v = None
    for cycle in range(2):
        if cycle == 0:
            v = wb
            remain = [KEEP * s + n for s, n in zip(source, neighbours(v, 1))]
        else:
            near = neighbours(v, 1)
            v = [KEEP * a + (c + w * n) for a, c, w, n in zip(v, wb, scale0, near)]
            near = neighbours(v, 1)
            remain = [(s - d * a) + n for s, d, a, n in zip(source, diag0, v, near)]
        coarse = middle_solve(block_mean(remain, 1), scale1, scale2)
        v = [a + c for a, c in zip(v, coarse)]
        near = neighbours(v, 1)
        v = [KEEP * a + (c + w * n) for a, c, w, n in zip(v, wb, scale0, near)]
    return v


def exact_dot(left, right):
    high = left.astype(BF16)
    rest = left - high.astype(F32)
    mid = rest.astype(BF16)
    low = (rest - mid.astype(F32)).astype(BF16)
    dot = functools.partial(jnp.dot, preferred_element_type=F32)
    return dot(high, right) + (dot(mid, right) + dot(low, right))


def spread(rows):
    own = (iota((CELLS, FACE), 1) >> 4) == iota((CELLS, FACE), 0)
    return jnp.concatenate([jnp.where(own, jnp.broadcast_to(r, (CELLS, FACE)), 0.0) for r in rows], axis=0)


def collect(field):
    own = (iota((CELLS, FACE), 1) >> 4) == iota((CELLS, FACE), 0)
    return [
        jnp.sum(jnp.where(own, field[CELLS * c : CELLS * c + CELLS], 0.0), axis=0, keepdims=True)
        for c in range(3)
    ]


def kernel(
    n_region,
    n_sub,
    multipliers,
    direction,
    residual,
    reaction,
    viscosity,
    primal_index,
    region_inverse,
    coarse_map,
    global_inverse,
    new_multipliers,
    new_residual,
    velocity,
    pressure,
    v_mult,
    v_dir,
    v_res,
    v_react,
    v_visc,
    v_index,
    v_rows,
    v_map,
    v_ginv,
    table,
    padded_index,
    halo,
    face_send,
    after,
    packet,
    gather,
    packet2,
    gather2,
    packet3,
    gather3,
    packet4,
    gather4,
    load_sem,
    halo_send,
    halo_recv,
    back_send,
    back_recv,
    sum_send,
    sum_recv,
):
    region = lax.axis_index("region")
    sub = lax.axis_index("sub")

    def sub_peer(i):
        return (region, lax.rem(sub + i, n_sub))

    def region_peer(i):
        return (lax.rem(region + i, n_region), sub)

    loads = [
        pltpu.make_async_copy(src, dst, load_sem.at[i])
        for i, (src, dst) in enumerate(
            (
                (direction, v_dir),
                (primal_index, v_index),
                (coarse_map, v_map),
                (residual, v_res),
                (reaction, v_react),
                (region_inverse, v_rows),
                (global_inverse, v_ginv),
                (multipliers, v_mult),
                (viscosity, v_visc),
            )
        )
    ]
    for load in loads:
        load.start()

    barrier = pltpu.get_barrier_semaphore()

    def greet_sub(i, carry):
        pl.semaphore_signal(barrier, inc=1, device_id=sub_peer(i), device_id_type=MESH)
        return carry

    def greet_region(i, carry):
        pl.semaphore_signal(barrier, inc=1, device_id=region_peer(i), device_id_type=MESH)
        return carry

    lax.fori_loop(1, n_sub, greet_sub, 0)
    lax.fori_loop(1, n_region, greet_region, 0)

    def send_all(src, dst_of_me, count, peer, index):
        def one(i, carry):
            pltpu.make_async_remote_copy(
                src_ref=src,
                dst_ref=dst_of_me,
                send_sem=sum_send.at[index],
                recv_sem=sum_recv.at[index],
                device_id=peer(i),
                device_id_type=MESH,
            ).start()
            return carry

        lax.fori_loop(1, count, one, 0)

    def all_of(buffer, count, peer, index):
        part = buffer.at[pl.ds(0, count - 1)]
        return pltpu.make_async_remote_copy(
            src_ref=part,
            dst_ref=part,
            send_sem=sum_send.at[index],
            recv_sem=sum_recv.at[index],
            device_id=peer(1),
            device_id_type=MESH,
        )

    row_i = iota((FACE, FACE), 0)
    col_i = iota((FACE, FACE), 1)
    table[0] = jnp.where((row_i & 15) == (col_i & 15), 1.0, 0.0).astype(BF16)
    table[1] = jnp.where((row_i & 15) == (col_i >> 4), 1.0, 0.0).astype(BF16)
    table[2] = jnp.where((row_i >> 4) == (col_i & 15), 1.0, 0.0).astype(BF16)

    loads[0].wait()
    loads[1].wait()
    padded_index[...] = jnp.full((8, 128), -1, jnp.int32)
    padded_index[0:1, 0:96] = v_index[...]
    index_row = padded_index[0:1, :]
    index_col = jnp.transpose(jnp.broadcast_to(index_row.astype(F32), (128, 128))).astype(jnp.int32)
    lane128 = iota((128, 128), 1)
    hit = jnp.where((index_col & 127) == lane128, 1.0, 0.0)
    key_col = index_col >> 7
    picked = jnp.zeros((128, 128), F32)
    for d in range(3):
        for c in range(3):
            for h in range(2):
                r = (d * 3 + c) * 2 + h
                values = v_dir[0, d, c : c + 1, 128 * h : 128 * h + 128]
                picked = jnp.where(key_col == r, jnp.broadcast_to(values, (128, 128)), picked)
    picked = picked * hit
    primal_row = jnp.sum(jnp.transpose(picked), axis=0, keepdims=True)
    primal_col = jnp.sum(picked, axis=1, keepdims=True)[:96]
    loads[2].wait()
    share = jnp.sum(primal_col * v_map[0], axis=0, keepdims=True)
    loads[3].wait()
    squares = jnp.sum(v_res[0] * v_res[0])
    lane_row = iota((1, 128), 1)
    packet[0:1, :] = jnp.where(lane_row < 96, primal_row, squares)
    for j in range(3):
        packet[j + 1 : j + 2, :] = share[:, 128 * j : 128 * j + 128]
    gather[sub] = packet[...]

    pl.semaphore_wait(barrier, n_sub - 1 + n_region - 1)

    above = (region_peer(1), sub_peer(DOM_Z), sub_peer(1))
    below = (region_peer(n_region - 1), sub_peer(n_sub - DOM_Z), sub_peer(n_sub - 1))
    faces = [
        pltpu.make_async_remote_copy(
            src_ref=v_dir.at[0, d],
            dst_ref=halo.at[d],
            send_sem=halo_send.at[d],
            recv_sem=halo_recv.at[d],
            device_id=above[d],
            device_id_type=MESH,
        )
        for d in (1, 2, 0)
    ]
    for copy in faces:
        copy.start()
    send_all(packet, gather.at[sub], n_sub, sub_peer, 0)

    lane = iota((CELLS, FACE), 1)
    y_lane = lane >> 4
    z_lane = lane & 15
    x_row = iota((CELLS, FACE), 0)
    same, to_z, from_z = 0, 1, 2

    def tile3(mask):
        return jnp.concatenate([mask] * 3, axis=0)

    def natural(face_rows, edge):
        in_y = exact_dot(spread(face_rows[1]), table[same])
        in_z = exact_dot(spread(face_rows[2]), table[to_z])
        blocks = []
        for c in range(3):
            part = jnp.where(x_row == edge, jnp.broadcast_to(face_rows[0][c], (CELLS, FACE)), 0.0)
            part = part + jnp.where(y_lane == edge, in_y[CELLS * c : CELLS * c + CELLS], 0.0)
            part = part + jnp.where(z_lane == edge, in_z[CELLS * c : CELLS * c + CELLS], 0.0)
            blocks.append(part)
        return jnp.concatenate(blocks, axis=0)

    upper = CELLS - 1
    own_faces = natural([[v_dir[0, d, c : c + 1, :] for c in range(3)] for d in range(3)], upper)
    loads[4].wait()
    react0 = split(v_react[0])
    react1 = block_mean(react0, 1)
    react2 = block_mean(react1, 2)
    diag0 = broad([r + 6.0 for r in react0])
    scale0 = broad([DAMPING / (r + 6.0) for r in react0])
    scale1 = broad([DAMPING / (r + 6.0 * 0.25) for r in react1])
    scale2 = [DAMPING / (r + 6.0 * 0.0625) for r in react2]

    for copy in faces:
        copy.wait_recv()
    under = natural([[halo[d, c : c + 1, :] for c in range(3)] for d in range(3)], 0)
    source = own_faces - under
    base = join(local_solve(split(source), diag0, scale0, scale1, scale2))

    def extract(edge):
        mask_y = tile3(y_lane == edge)
        mask_z = tile3(z_lane == edge)
        in_y = collect(exact_dot(jnp.where(mask_y, base, 0.0), table[same]))
        in_z = collect(exact_dot(jnp.where(mask_z, base, 0.0), table[from_z]))
        in_x = [base[CELLS * c + edge : CELLS * c + edge + 1] for c in range(3)]
        return [in_x, in_y, in_z]

    lower_rows = extract(0)
    for d in range(3):
        for c in range(3):
            face_send[d, c : c + 1, :] = lower_rows[d][c]
    backs = [
        pltpu.make_async_remote_copy(
            src_ref=face_send.at[d],
            dst_ref=after.at[d],
            send_sem=back_send.at[d],
            recv_sem=back_recv.at[d],
            device_id=below[d],
            device_id_type=MESH,
        )
        for d in (1, 2, 0)
    ]
    for copy in backs:
        copy.start()

    all_of(gather, n_sub, sub_peer, 0).wait_recv()
    everyone = gather[...]
    packet2[...] = jnp.sum(everyone, axis=0)
    gather2[region] = packet2[...]
    send_all(packet2, gather2.at[region], n_region, region_peer, 1)
    loads[5].wait()
    rows_y = n_sub // DOM_Z
    lane_a = iota((rows_y, 128), 1)
    quads = []
    for b in range(DOM_Z):
        quads.append(jnp.concatenate([gather[DOM_Z * a + b, 0:1, :] for a in range(rows_y)], axis=0))

    def shifted(v, by):
        return pltpu.roll(v, by % 128, 1) if by % 128 else v

    packed = [
        jnp.where(lane_a < 96, quads[0], shifted(quads[1], 96)),
        jnp.where(lane_a < 64, shifted(quads[1], -32), shifted(quads[2], 64)),
        jnp.where(lane_a < 32, shifted(quads[2], -64), shifted(quads[3], 32)),
    ]
    lanes = jnp.zeros((96, 128), F32)
    for a in range(rows_y):
        for j in range(3):
            at = (3 * a + j) * 128
            lanes = lanes + v_rows[0, :, at : at + 128] * packed[j][a : a + 1, :]

    def lane_total(v):
        tall = jnp.concatenate([v, jnp.zeros((32, 128), F32)], axis=0)
        return jnp.sum(jnp.transpose(tall), axis=0, keepdims=True)

    region_row = lane_total(lanes)
    part = jnp.sum(source * base, axis=0, keepdims=True)
    part = part[:, :128] + part[:, 128:] + primal_row * region_row
    packet3[...] = jnp.broadcast_to(part, (8, 128))
    gather3[sub] = packet3[...]
    send_all(packet3, gather3.at[sub], n_sub, sub_peer, 2)

    all_of(gather2, n_region, region_peer, 1).wait_recv()
    whole = jnp.sum(gather2[...], axis=0)
    squares_all = jnp.sum(jnp.where(lane_row == 96, whole[0:1, :], 0.0))
    total = jnp.concatenate([whole[1:2, :], whole[2:3, :], whole[3:4, :]], axis=1)
    loads[6].wait()
    top = lax.dot_general(
        jnp.broadcast_to(total, (8, 384)),
        v_ginv[...],
        (((1,), (1,)), ((), ())),
        precision=lax.Precision.HIGHEST,
        preferred_element_type=F32,
    )[0:1]
    energy = jnp.sum(total * top)
    weighted = v_map[0] * top
    lanes = weighted[:, :128] + weighted[:, 128:256] + weighted[:, 256:]
    lifted = region_row + lane_total(lanes)
    key_row = jnp.broadcast_to(index_row >> 7, (32, 128))
    placed = jnp.where(key_row == iota((32, 128), 0), jnp.broadcast_to(lifted, (32, 128)), 0.0)
    placed = exact_dot(placed, hit.astype(BF16))

    def lifted_row(d, c):
        r = (d * 3 + c) * 2
        return jnp.concatenate([placed[r : r + 1], placed[r + 1 : r + 2]], axis=1)

    lifted_rows = [[lifted_row(d, c) for c in range(3)] for d in range(3)]
    field = base + natural(lifted_rows, upper)
    upper_rows = extract(upper)
    for c in range(3):
        velocity[0, c] = field[CELLS * c : CELLS * c + CELLS]

    all_of(gather3, n_sub, sub_peer, 2).wait_recv()
    packet4[...] = jnp.sum(gather3[...], axis=0)
    gather4[region] = packet4[...]
    send_all(packet4, gather4.at[region], n_region, region_peer, 3)

    for copy in backs:
        copy.wait_recv()
    loads[7].wait()
    loads[8].wait()
    v = [field[CELLS * c : CELLS * c + CELLS] for c in range(3)]
    edge_x = jnp.broadcast_to(after[0, 0:1, :], (CELLS, FACE))
    edge_y = exact_dot(spread([after[1, 1:2, :]]), table[same])
    edge_z = exact_dot(spread([after[2, 2:3, :]]), table[to_z])
    step_x = jnp.where(x_row == upper, edge_x, pltpu.roll(v[0], CELLS - 1, 0)) - v[0]
    step_y = jnp.where(y_lane == upper, edge_y, pltpu.roll(v[1], FACE - CELLS, 1)) - v[1]
    step_z = jnp.where(z_lane == upper, edge_z, pltpu.roll(v[2], FACE - 1, 1)) - v[2]
    pressure[0] = -v_visc[0] * (step_x + step_y + step_z)
    jumps = []
    for d in range(3):
        rows = [upper_rows[d][c] + lifted_rows[d][c] for c in range(3)]
        jumps.append(jnp.concatenate(rows, axis=0) - after[d])

    all_of(gather4, n_region, region_peer, 3).wait_recv()
    curvature = jnp.sum(jnp.sum(gather4[...], axis=0)[0:1]) + energy
    alpha = squares_all / curvature
    for d in range(3):
        new_multipliers[0, d] = v_mult[0, d] + alpha * v_dir[0, d]
        new_residual[0, d] = v_res[0, d] - alpha * jumps[d]

    for copy in faces:
        copy.wait_send()
    for copy in backs:
        copy.wait_send()
    all_of(gather, n_sub, sub_peer, 0).wait_send()
    all_of(gather2, n_region, region_peer, 1).wait_send()
    all_of(gather3, n_sub, sub_peer, 2).wait_send()
    all_of(gather4, n_region, region_peer, 3).wait_send()


def solution(mesh):
    n_region = mesh.shape["region"]
    n_sub = mesh.shape["sub"]

    def body(*args):
        shapes = [a.shape for a in args]
        vmem = [pltpu.VMEM(a.shape, a.dtype) for a in args[:8]] + [pltpu.VMEM(args[8].shape, F32)]
        like = (args[0], args[2])
        outs = [jax.ShapeDtypeStruct(a.shape, F32) for a in like]
        outs.append(jax.ShapeDtypeStruct((1, 3, CELLS, FACE), F32))
        outs.append(jax.ShapeDtypeStruct((1, CELLS, FACE), F32))
        return tuple(
            pl.pallas_call(
                functools.partial(kernel, n_region, n_sub),
                out_shape=outs,
                in_specs=[pl.BlockSpec(memory_space=pl.ANY)] * 9,
                out_specs=[pl.BlockSpec(memory_space=pltpu.VMEM)] * 4,
                scratch_shapes=vmem
                + [
                    pltpu.VMEM((3, FACE, FACE), BF16),
                    pltpu.VMEM((8, 128), jnp.int32),
                    pltpu.VMEM((3, 3, FACE), F32),
                    pltpu.VMEM((3, 3, FACE), F32),
                    pltpu.VMEM((3, 3, FACE), F32),
                    pltpu.VMEM((4, 128), F32),
                    pltpu.VMEM((n_sub, 4, 128), F32),
                    pltpu.VMEM((4, 128), F32),
                    pltpu.VMEM((n_region, 4, 128), F32),
                    pltpu.VMEM((8, 128), F32),
                    pltpu.VMEM((n_sub, 8, 128), F32),
                    pltpu.VMEM((8, 128), F32),
                    pltpu.VMEM((n_region, 8, 128), F32),
                    pltpu.SemaphoreType.DMA((9,)),
                    pltpu.SemaphoreType.DMA((3,)),
                    pltpu.SemaphoreType.DMA((3,)),
                    pltpu.SemaphoreType.DMA((3,)),
                    pltpu.SemaphoreType.DMA((3,)),
                    pltpu.SemaphoreType.DMA((4,)),
                    pltpu.SemaphoreType.DMA((4,)),
                ],
                compiler_params=pltpu.CompilerParams(collective_id=0, has_side_effects=True),
                name="feti",
            )(*args)
        )

    in_specs = (
        P(("region", "sub"), None, None, None),
        P(("region", "sub"), None, None, None),
        P(("region", "sub"), None, None, None),
        P(("region", "sub"), None, None),
        P(("region", "sub"), None, None),
        P(("region", "sub"), None),
        P("region", "sub", None),
        P(("region", "sub"), None, None),
        P(),
    )
    out_specs = (
        P(("region", "sub"), None, None, None),
        P(("region", "sub"), None, None, None),
        P(("region", "sub"), None, None, None),
        P(("region", "sub"), None, None),
    )
    return jax.shard_map(body, mesh=mesh, in_specs=in_specs, out_specs=out_specs, check_vma=False)
```

time: 371 us -> 41.7 us (0.11)
  blocking collectives: 289 us -> 0 us
  Pallas kernels: 0 us -> 31.2 us
  other arithmetic: 29.4 us -> 0 us
  local copies, waits for them, and re-layouts: 27.2 us -> 9.28 us
  starting transfers between devices: 14.8 us -> 0 us
    psum x2 -> x0, blocking collectives: 174 us -> none  [the longest x1 100 us: body(): total = lax.psum(share, ('region', 'sub'))]
    unnamed x1 -> x0, blocking collectives: 115 us -> none
    pallas_call x0 -> x1, Pallas kernels: none -> 31.2 us  [body(): pl.pallas_call(functools.partial(kernel, n_region, n_sub), out_shape=outs...]
    ppermute x6 -> x0, starting transfers between devices: 14.8 us -> none  [shifted_2(): return lax.ppermute(x, axis, [(i, (i + by) % count) for i in range(count)])]
    reshape x20 -> x0, local copies, waits for them, and re-layouts: 12.1 us -> none  [the longest x4 10.7 us: restrict(): array.reshape(lead + (depth // 2, 2, half, 2, half, 2))]
    add x26 -> x0, other arithmetic: 10.1 us -> none  [the longest x17 7.44 us: relax(): field + damping * (source - operate(field, react, weight, cells)) / diagonal]
    reduce_sum x8 -> x0, other arithmetic: 6.22 us -> none  [the longest x6 5 us: restrict(): array.reshape(lead + (depth // 2, 2, half, 2, half, 2))]
    unnamed x29 -> x5, local copies, waits for them, and re-layouts: 1.92 us -> 6.65 us
  transfers between devices with their start and end apart: 6 -> 0, of which waited for: 1 -> 0; matrix products, arithmetic and copies ran while one was open for 4% -> 0% of each run, Pallas kernels for 0% -> 0%
where the time goes in v1:
time: 41.7 us; the launch traced here: 41.1 us
  Pallas kernels  31.2 us (75%)
  local copies, waits for them, and re-layouts  9.28 us (22%)
  between operations  0.64 us (2%)
    pallas_call x1, Pallas kernels, body(): pl.pallas_call(functools.partial(kernel, n_region, n_sub), out_shape=outs...  31.2 us
    unnamed x5, local copies, waits for them, and re-layouts  6.65 us
    pallas_call x2, local copies, waits for them, and re-layouts, body(): pl.pallas_call(functools.partial(kernel, n_region, n_sub), out_shape=outs...  2.63 us

profile of v1, /device:TPU:1, one launch (start us, length us, event | category | flops | bytes accessed | tf_op | source)
XLA Modules:
  0.0 41.1 jit_solution(9479152879203759229)
XLA Ops:
  0.6 1.3 %copy.13.multipliers = f32[1,3,3,256]{3,2,1,0:T(4,128)} copy(f32[1,3,3,256]{3,0,2,1:T(1,128)} %param.9) | data formatting | bytes 18432 | tf_op args[0]
  1.9 1.3 %copy.14.direction = f32[1,3,3,256]{3,2,1,0:T(4,128)} copy(f32[1,3,3,256]{3,0,2,1:T(1,128)} %param.10) | data formatting | bytes 18432 | tf_op args[1]
  3.2 1.3 %copy.15.residual = f32[1,3,3,256]{3,2,1,0:T(4,128)} copy(f32[1,3,3,256]{3,0,2,1:T(1,128)} %param.11) | data formatting | bytes 18432 | tf_op args[2]
  4.5 31.2 %feti.1 = (f32[1,3,3,256]{3,2,1,0:T(4,128)}, f32[1,3,3,256]{3,2,1,0:T(4,128)}, f32[1,3,16,256]{3,2,1,0:T(8,128)}, f32[1,16,256]{2,1,0:T(8,128)}) custom-call(f32[1,3,3,256]{3,2,1,0:T(4,128)} %copy.13.multipliers, f32[1,3,3,256]{3,2,1,0:T(4,128)} %copy.14.direction, f32[1,3,3,256]{3,2,1,0:T(4,128)} %copy.15.residual, f32[1,16,256]{2,1,0:T(8,128)} %reaction.1, ...), custom_call_target="tpu_custom_call" | custom-call | tf_op jit(solution)/shard_map/feti/pallas_call | solution.py:522
  35.8 1.3 %copy.16 = f32[1,3,3,256]{3,0,2,1:T(1,128)} copy(f32[1,3,3,256]{3,2,1,0:T(4,128)} %get-tuple-element.4) | data formatting | bytes 18432 | tf_op jit(solution)/shard_map/feti/pallas_call | solution.py:522
  37.1 1.3 %copy.17 = f32[1,3,3,256]{3,0,2,1:T(1,128)} copy(f32[1,3,3,256]{3,2,1,0:T(4,128)} %get-tuple-element.5) | data formatting | bytes 18432 | tf_op jit(solution)/shard_map/feti/pallas_call | solution.py:522
  38.4 1.4 %copy.20 = f32[1,3,16,256]{3,2,1,0:T(8,128)} copy(f32[1,3,16,256]{3,2,1,0:T(8,128)} %get-tuple-element.14) | data formatting | bytes 98304
  39.8 1.3 %copy.21 = f32[1,16,256]{2,1,0:T(8,128)} copy(f32[1,16,256]{2,1,0:T(8,128)} %get-tuple-element.15) | data formatting | bytes 32768

commit v2 on v1

--- a/solution.py
+++ b/solution.py
@@ -12,6 +12,7 @@
 CELLS = 16
 FACE = 256
 DAMPING = 0.8
+VMEM_LIMIT = 16 * 1024 * 1024
 KEEP = 0.2
 MESH = pl.DeviceIdType.MESH
 F32 = jnp.float32
@@ -175,7 +176,6 @@
 def kernel(
     n_region,
     n_sub,
-    multipliers,
     direction,
     residual,
     reaction,
@@ -184,11 +184,10 @@
     region_inverse,
     coarse_map,
     global_inverse,
-    new_multipliers,
-    new_residual,
+    jump,
+    alpha,
     velocity,
     pressure,
-    v_mult,
     v_dir,
     v_res,
     v_react,
@@ -238,7 +237,6 @@
                 (reaction, v_react),
                 (region_inverse, v_rows),
                 (global_inverse, v_ginv),
-                (multipliers, v_mult),
                 (viscosity, v_visc),
             )
         )
@@ -304,7 +302,7 @@
         for c in range(3):
             for h in range(2):
                 r = (d * 3 + c) * 2 + h
-                values = v_dir[0, d, c : c + 1, 128 * h : 128 * h + 128]
+                values = v_dir[d, c, :, 128 * h : 128 * h + 128]
                 picked = jnp.where(key_col == r, jnp.broadcast_to(values, (128, 128)), picked)
     picked = picked * hit
     primal_row = jnp.sum(jnp.transpose(picked), axis=0, keepdims=True)
@@ -312,7 +310,7 @@
     loads[2].wait()
     share = jnp.sum(primal_col * v_map[0], axis=0, keepdims=True)
     loads[3].wait()
-    squares = jnp.sum(v_res[0] * v_res[0])
+    squares = jnp.sum(v_res[...] * v_res[...])
     lane_row = iota((1, 128), 1)
     packet[0:1, :] = jnp.where(lane_row < 96, primal_row, squares)
     for j in range(3):
@@ -325,7 +323,7 @@
     below = (region_peer(n_region - 1), sub_peer(n_sub - DOM_Z), sub_peer(n_sub - 1))
     faces = [
         pltpu.make_async_remote_copy(
-            src_ref=v_dir.at[0, d],
+            src_ref=v_dir.at[d],
             dst_ref=halo.at[d],
             send_sem=halo_send.at[d],
             recv_sem=halo_recv.at[d],
@@ -359,7 +357,7 @@
         return jnp.concatenate(blocks, axis=0)
 
     upper = CELLS - 1
-    own_faces = natural([[v_dir[0, d, c : c + 1, :] for c in range(3)] for d in range(3)], upper)
+    own_faces = natural([[v_dir[d, c] for c in range(3)] for d in range(3)], upper)
     loads[4].wait()
     react0 = split(v_react[0])
     react1 = block_mean(react0, 1)
@@ -371,7 +369,7 @@
 
     for copy in faces:
         copy.wait_recv()
-    under = natural([[halo[d, c : c + 1, :] for c in range(3)] for d in range(3)], 0)
+    under = natural([[halo[d, c] for c in range(3)] for d in range(3)], 0)
     source = own_faces - under
     base = join(local_solve(split(source), diag0, scale0, scale1, scale2))
 
@@ -386,7 +384,7 @@
     lower_rows = extract(0)
     for d in range(3):
         for c in range(3):
-            face_send[d, c : c + 1, :] = lower_rows[d][c]
+            face_send[d, c] = lower_rows[d][c]
     backs = [
         pltpu.make_async_remote_copy(
             src_ref=face_send.at[d],
@@ -476,26 +474,21 @@
     for copy in backs:
         copy.wait_recv()
     loads[7].wait()
-    loads[8].wait()
     v = [field[CELLS * c : CELLS * c + CELLS] for c in range(3)]
-    edge_x = jnp.broadcast_to(after[0, 0:1, :], (CELLS, FACE))
-    edge_y = exact_dot(spread([after[1, 1:2, :]]), table[same])
-    edge_z = exact_dot(spread([after[2, 2:3, :]]), table[to_z])
+    edge_x = jnp.broadcast_to(after[0, 0], (CELLS, FACE))
+    edge_y = exact_dot(spread([after[1, 1]]), table[same])
+    edge_z = exact_dot(spread([after[2, 2]]), table[to_z])
     step_x = jnp.where(x_row == upper, edge_x, pltpu.roll(v[0], CELLS - 1, 0)) - v[0]
     step_y = jnp.where(y_lane == upper, edge_y, pltpu.roll(v[1], FACE - CELLS, 1)) - v[1]
     step_z = jnp.where(z_lane == upper, edge_z, pltpu.roll(v[2], FACE - 1, 1)) - v[2]
     pressure[0] = -v_visc[0] * (step_x + step_y + step_z)
-    jumps = []
     for d in range(3):
-        rows = [upper_rows[d][c] + lifted_rows[d][c] for c in range(3)]
-        jumps.append(jnp.concatenate(rows, axis=0) - after[d])
+        for c in range(3):
+            jump[d, c] = upper_rows[d][c] + lifted_rows[d][c] - after[d, c]
 
     all_of(gather4, n_region, region_peer, 3).wait_recv()
     curvature = jnp.sum(jnp.sum(gather4[...], axis=0)[0:1]) + energy
-    alpha = squares_all / curvature
-    for d in range(3):
-        new_multipliers[0, d] = v_mult[0, d] + alpha * v_dir[0, d]
-        new_residual[0, d] = v_res[0, d] - alpha * jumps[d]
+    alpha[...] = jnp.broadcast_to(squares_all / curvature, (8, 128))
 
     for copy in faces:
         copy.wait_send()
@@ -507,50 +500,70 @@
     all_of(gather4, n_region, region_peer, 3).wait_send()
 
 
+def finish(multipliers, direction, residual, jump, alpha, velocity, pressure, *outs):
+    step = jnp.broadcast_to(alpha[0:1, 0:1], (1, FACE))
+    for d in range(3):
+        for c in range(3):
+            outs[0][d, c] = multipliers[d, c] + step * direction[d, c]
+            outs[1][d, c] = residual[d, c] - step * jump[d, c]
+    outs[2][...] = velocity[...]
+    outs[3][...] = pressure[...]
+
+
 def solution(mesh):
     n_region = mesh.shape["region"]
     n_sub = mesh.shape["sub"]
 
-    def body(*args):
-        shapes = [a.shape for a in args]
-        vmem = [pltpu.VMEM(a.shape, a.dtype) for a in args[:8]] + [pltpu.VMEM(args[8].shape, F32)]
-        like = (args[0], args[2])
-        outs = [jax.ShapeDtypeStruct(a.shape, F32) for a in like]
-        outs.append(jax.ShapeDtypeStruct((1, 3, CELLS, FACE), F32))
-        outs.append(jax.ShapeDtypeStruct((1, CELLS, FACE), F32))
-        return tuple(
-            pl.pallas_call(
-                functools.partial(kernel, n_region, n_sub),
-                out_shape=outs,
-                in_specs=[pl.BlockSpec(memory_space=pl.ANY)] * 9,
-                out_specs=[pl.BlockSpec(memory_space=pltpu.VMEM)] * 4,
-                scratch_shapes=vmem
-                + [
-                    pltpu.VMEM((3, FACE, FACE), BF16),
-                    pltpu.VMEM((8, 128), jnp.int32),
-                    pltpu.VMEM((3, 3, FACE), F32),
-                    pltpu.VMEM((3, 3, FACE), F32),
-                    pltpu.VMEM((3, 3, FACE), F32),
-                    pltpu.VMEM((4, 128), F32),
-                    pltpu.VMEM((n_sub, 4, 128), F32),
-                    pltpu.VMEM((4, 128), F32),
-                    pltpu.VMEM((n_region, 4, 128), F32),
-                    pltpu.VMEM((8, 128), F32),
-                    pltpu.VMEM((n_sub, 8, 128), F32),
-                    pltpu.VMEM((8, 128), F32),
-                    pltpu.VMEM((n_region, 8, 128), F32),
-                    pltpu.SemaphoreType.DMA((9,)),
-                    pltpu.SemaphoreType.DMA((3,)),
-                    pltpu.SemaphoreType.DMA((3,)),
-                    pltpu.SemaphoreType.DMA((3,)),
-                    pltpu.SemaphoreType.DMA((3,)),
-                    pltpu.SemaphoreType.DMA((4,)),
-                    pltpu.SemaphoreType.DMA((4,)),
-                ],
-                compiler_params=pltpu.CompilerParams(collective_id=0, has_side_effects=True),
-                name="feti",
-            )(*args)
+    def body(multipliers, direction, residual, *rest):
+        faces = [a.reshape(3, 3, 1, FACE) for a in (multipliers, direction, residual)]
+        args = [pltpu.with_memory_space_constraint(a, pltpu.HBM) for a in (faces[1], faces[2]) + rest]
+        face = jax.ShapeDtypeStruct((3, 3, 1, FACE), F32)
+        cells = jax.ShapeDtypeStruct((1, 3, CELLS, FACE), F32)
+        scalar_cells = jax.ShapeDtypeStruct((1, CELLS, FACE), F32)
+        inner = pl.pallas_call(
+            functools.partial(kernel, n_region, n_sub),
+            out_shape=[face, jax.ShapeDtypeStruct((8, 128), F32), cells, scalar_cells],
+            in_specs=[pl.BlockSpec(memory_space=pltpu.HBM)] * 8,
+            out_specs=[pl.BlockSpec(memory_space=pltpu.VMEM)] * 4,
+            scratch_shapes=[pltpu.VMEM(a.shape, a.dtype) for a in args]
+            + [
+                pltpu.VMEM((3, FACE, FACE), BF16),
+                pltpu.VMEM((8, 128), jnp.int32),
+                pltpu.VMEM((3, 3, 1, FACE), F32),
+                pltpu.VMEM((3, 3, 1, FACE), F32),
+                pltpu.VMEM((3, 3, 1, FACE), F32),
+                pltpu.VMEM((4, 128), F32),
+                pltpu.VMEM((n_sub, 4, 128), F32),
+                pltpu.VMEM((4, 128), F32),
+                pltpu.VMEM((n_region, 4, 128), F32),
+                pltpu.VMEM((8, 128), F32),
+                pltpu.VMEM((n_sub, 8, 128), F32),
+                pltpu.VMEM((8, 128), F32),
+                pltpu.VMEM((n_region, 8, 128), F32),
+                pltpu.SemaphoreType.DMA((8,)),
+                pltpu.SemaphoreType.DMA((3,)),
+                pltpu.SemaphoreType.DMA((3,)),
+                pltpu.SemaphoreType.DMA((3,)),
+                pltpu.SemaphoreType.DMA((3,)),
+                pltpu.SemaphoreType.DMA((4,)),
+                pltpu.SemaphoreType.DMA((4,)),
+            ],
+            compiler_params=pltpu.CompilerParams(
+                collective_id=0, has_side_effects=True, vmem_limit_bytes=VMEM_LIMIT
+            ),
+            name="feti",
         )
+        jump, alpha, velocity, pressure = inner(*args)
+        outs = pl.pallas_call(
+            finish,
+            out_shape=[face, face, cells, scalar_cells],
+            in_specs=[pl.BlockSpec(memory_space=pltpu.VMEM)] * 7,
+            out_specs=[pl.BlockSpec(memory_space=pltpu.VMEM)] * 4,
+            compiler_params=pltpu.CompilerParams(vmem_limit_bytes=VMEM_LIMIT),
+            name="finish",
+        )(*faces, jump, alpha, velocity, pressure)
+        shape = multipliers.shape
+        return outs[0].reshape(shape), outs[1].reshape(shape), outs[2], outs[3]
 
     in_specs = (
         P(("region", "sub"), None, None, None),

time: 41.7 us -> 32.2 us (0.77); the launches traced: 41.1 us -> 32.1 us
  local copies, waits for them, and re-layouts: 9.28 us -> 0.01 us
    unnamed x5 -> x6, local copies, waits for them, and re-layouts: 6.65 us -> 0.01 us
    pallas_call x2 -> x0, local copies, waits for them, and re-layouts: 2.63 us -> none  [body(): pl.pallas_call(functools.partial(kernel, n_region, n_sub), out_shape=outs...]
    pallas_call x1 -> x2, Pallas kernels: 31.2 us -> 31.4 us  [the longest x1 30.7 us: body(): jump, alpha, velocity, pressure = inner(*args)]
where the time goes in v2:
time: 32.2 us; the launch traced here: 32.1 us
  Pallas kernels  31.4 us (98%)
  between operations  0.69 us (2%)
    pallas_call x1, Pallas kernels, body(): jump, alpha, velocity, pressure = inner(*args)  30.7 us
    pallas_call x1, Pallas kernels, body(): pl.pallas_call(finish, out_shape=[face, face, cells, scalar_cells], in_sp...  0.71 us

profile of v2, /device:TPU:1, one launch (start us, length us, event | category | flops | bytes accessed | tf_op | source)
XLA Modules:
  0.0 32.1 jit_solution(9877170433409217516)
XLA Ops:
  0.6 0.0 copy-start.1
  0.6 0.0 copy-start
  0.7 0.0 copy-start.2
  0.7 30.7 %feti.1 = (f32[3,3,1,256]{3,2,1,0:T(1,128)S(1)}, f32[8,128]{1,0:T(8,128)S(1)}, f32[1,3,16,256]{3,2,1,0:T(8,128)S(1)}, f32[1,16,256]{2,1,0:T(8,128)S(1)}) custom-call(f32[3,3,1,256]{3,2,1,0:T(1,128)} %bitcast.5, f32[3,3,1,256]{3,2,1,0:T(1,128)} %bitcast.7, f32[1,16,256]{2,1,0:T(8,128)} %reaction.1, f32[1,16,256]{2,1,0:T(8,128)} %viscosity.1, ...), custom_call_target="tpu_custom_call" | custom-call | tf_op jit(solution)/shard_map/feti/pallas_call | solution.py:556
  31.4 0.0 copy-done.1
  31.4 0.0 copy-done
  31.4 0.0 copy-done.2
  31.4 0.7 %finish.1 = (f32[3,3,1,256]{3,2,1,0:T(1,128)}, f32[3,3,1,256]{3,2,1,0:T(1,128)}, f32[1,3,16,256]{3,2,1,0:T(8,128)}, f32[1,16,256]{2,1,0:T(8,128)}) custom-call(f32[3,3,1,256]{3,2,1,0:T(1,128)S(1)} %bitcast.9, f32[3,3,1,256]{3,2,1,0:T(1,128)S(1)} %bitcast.6, f32[3,3,1,256]{3,2,1,0:T(1,128)S(1)} %bitcast.8, f32[3,3,1,256]{3,2,1,0:T(1,128)S(1)} %get-tuple-element.12.jump, ...), custom_call_target="tpu_custom_call" | custom-call | tf_op jit(solution)/shard_map/finish/pallas_call | solution.py:557
Async XLA Ops:
  0.6 30.8 %copy-start.1 = (f32[1,3,3,256]{3,0,2,1:T(1,128)S(1)}, f32[1,3,3,256]{3,0,2,1:T(1,128)}, u32[]{:S(2)}) copy-start(f32[1,3,3,256]{3,0,2,1:T(1,128)} %param.11) | copy-start | bytes 27652
  0.6 30.8 %copy-start = (f32[1,3,3,256]{3,0,2,1:T(1,128)S(1)}, f32[1,3,3,256]{3,0,2,1:T(1,128)}, u32[]{:S(2)}) copy-start(f32[1,3,3,256]{3,0,2,1:T(1,128)} %param.10) | copy-start | bytes 27652
  0.7 30.8 %copy-start.2 = (f32[1,3,3,256]{3,0,2,1:T(1,128)S(1)}, f32[1,3,3,256]{3,0,2,1:T(1,128)}, u32[]{:S(2)}) copy-start(f32[1,3,3,256]{3,0,2,1:T(1,128)} %param.9) | copy-start | bytes 27652

commit v3 on v2

--- a/solution.py
+++ b/solution.py
@@ -8,6 +8,7 @@
 from jax.sharding import PartitionSpec as P
 
 DOM_Z = 4
+Z_LINE = 8
 COARSE_SWEEPS = 8
 CELLS = 16
 FACE = 256
@@ -202,13 +203,13 @@
     face_send,
     after,
     packet,
+    gather_y,
+    block,
     gather,
     packet2,
     gather2,
     packet3,
     gather3,
-    packet4,
-    gather4,
     load_sem,
     halo_send,
     halo_recv,
@@ -220,11 +221,21 @@
     region = lax.axis_index("region")
     sub = lax.axis_index("sub")
 
+    n_y = n_sub // Z_LINE
+    at_y = sub // Z_LINE
+    at_z = lax.rem(sub, Z_LINE)
+
     def sub_peer(i):
         return (region, lax.rem(sub + i, n_sub))
 
     def region_peer(i):
         return (lax.rem(region + i, n_region), sub)
+
+    def y_peer(i):
+        return (region, lax.rem(at_y + i, n_y) * Z_LINE + at_z)
+
+    def z_peer(i):
+        return (region, at_y * Z_LINE + lax.rem(at_z + i, Z_LINE))
 
     loads = [
         pltpu.make_async_copy(src, dst, load_sem.at[i])
@@ -246,41 +257,55 @@
 
     barrier = pltpu.get_barrier_semaphore()
 
-    def greet_sub(i, carry):
-        pl.semaphore_signal(barrier, inc=1, device_id=sub_peer(i), device_id_type=MESH)
-        return carry
-
-    def greet_region(i, carry):
-        pl.semaphore_signal(barrier, inc=1, device_id=region_peer(i), device_id_type=MESH)
-        return carry
-
-    lax.fori_loop(1, n_sub, greet_sub, 0)
-    lax.fori_loop(1, n_region, greet_region, 0)
-
-    def send_all(src, dst_of_me, count, peer, index):
-        def one(i, carry):
+    near = [sub_peer(n_sub - DOM_Z), sub_peer(n_sub - 1), sub_peer(DOM_Z), sub_peer(1)]
+    near += [z_peer(i) for i in range(1, Z_LINE)]
+    near += [y_peer(i) for i in range(1, n_y)] + [region_peer(i) for i in range(1, n_region)]
+    for peer in near:
+        pl.semaphore_signal(barrier, inc=1, device_id=peer, device_id_type=MESH)
+
+    def send_all(src, dst_of_me, peers, index):
+        for peer in peers:
             pltpu.make_async_remote_copy(
                 src_ref=src,
                 dst_ref=dst_of_me,
                 send_sem=sum_send.at[index],
                 recv_sem=sum_recv.at[index],
-                device_id=peer(i),
+                device_id=peer,
                 device_id_type=MESH,
             ).start()
-            return carry
-
-        lax.fori_loop(1, count, one, 0)
-
-    def all_of(buffer, count, peer, index):
-        part = buffer.at[pl.ds(0, count - 1)]
+
+    def all_of(buffer, peers, index):
+        part = buffer.at[pl.ds(0, len(peers))]
         return pltpu.make_async_remote_copy(
             src_ref=part,
             dst_ref=part,
             send_sem=sum_send.at[index],
             recv_sem=sum_recv.at[index],
-            device_id=peer(1),
+            device_id=peers[0],
             device_id_type=MESH,
         )
+
+    on_y = [y_peer(i) for i in range(1, n_y)]
+    on_z = [z_peer(i) for i in range(1, Z_LINE)]
+    on_region = [region_peer(i) for i in range(1, n_region)]
+
+    at_x = region // 2
+    at_c = lax.rem(region, 2)
+    n_x = n_region // 2
+    found = []
+    for dx in range(n_x):
+        for dc in range(2):
+            for dy in range(n_y):
+                for dz in range(Z_LINE):
+                    if dx or dc or dy or dz:
+                        hops = min(dx, n_x - dx) + min(dy, n_y - dy) + min(dz, Z_LINE - dz)
+                        found.append((-hops, dx, dc, dy, dz))
+    found.sort()
+    xs = [lax.rem(at_x + i, n_x) * 2 for i in range(n_x)]
+    cs = [lax.rem(at_c + i, 2) for i in range(2)]
+    ys = [lax.rem(at_y + i, n_y) * Z_LINE for i in range(n_y)]
+    zs = [lax.rem(at_z + i, Z_LINE) for i in range(Z_LINE)]
+    everyone = [(xs[dx] + cs[dc], ys[dy] + zs[dz]) for _, dx, dc, dy, dz in found]
 
     row_i = iota((FACE, FACE), 0)
     col_i = iota((FACE, FACE), 1)
@@ -289,6 +314,21 @@
     table[2] = jnp.where((row_i >> 4) == (col_i & 15), 1.0, 0.0).astype(BF16)
 
     loads[0].wait()
+    pl.semaphore_wait(barrier, len(near))
+
+    def face_copy(src, dst, send, recv, peer):
+        return pltpu.make_async_remote_copy(
+            src_ref=src, dst_ref=dst, send_sem=send, recv_sem=recv, device_id=peer, device_id_type=MESH
+        )
+
+    below = (region_peer(n_region - 1), sub_peer(n_sub - DOM_Z), sub_peer(n_sub - 1))
+    faces = [
+        face_copy(v_dir.at[1], halo.at[1], halo_send.at[1], halo_recv.at[1], sub_peer(DOM_Z)),
+        face_copy(v_dir.at[2], halo.at[2], halo_send.at[2], halo_recv.at[2], sub_peer(1)),
+        face_copy(v_dir.at[0], halo.at[0], halo_send.at[0], halo_recv.at[0], region_peer(1)),
+    ]
+    for copy in faces:
+        copy.start()
     loads[1].wait()
     padded_index[...] = jnp.full((8, 128), -1, jnp.int32)
     padded_index[0:1, 0:96] = v_index[...]
@@ -315,27 +355,9 @@
     packet[0:1, :] = jnp.where(lane_row < 96, primal_row, squares)
     for j in range(3):
         packet[j + 1 : j + 2, :] = share[:, 128 * j : 128 * j + 128]
-    gather[sub] = packet[...]
-
-    pl.semaphore_wait(barrier, n_sub - 1 + n_region - 1)
-
-    above = (region_peer(1), sub_peer(DOM_Z), sub_peer(1))
-    below = (region_peer(n_region - 1), sub_peer(n_sub - DOM_Z), sub_peer(n_sub - 1))
-    faces = [
-        pltpu.make_async_remote_copy(
-            src_ref=v_dir.at[d],
-            dst_ref=halo.at[d],
-            send_sem=halo_send.at[d],
-            recv_sem=halo_recv.at[d],
-            device_id=above[d],
-            device_id_type=MESH,
-        )
-        for d in (1, 2, 0)
-    ]
-    for copy in faces:
-        copy.start()
-    send_all(packet, gather.at[sub], n_sub, sub_peer, 0)
-
+    gather_y[at_y] = packet[...]
+
+    send_all(packet, gather_y.at[at_y], on_y, 0)
     lane = iota((CELLS, FACE), 1)
     y_lane = lane >> 4
     z_lane = lane & 15
@@ -367,11 +389,59 @@
     scale1 = broad([DAMPING / (r + 6.0 * 0.25) for r in react1])
     scale2 = [DAMPING / (r + 6.0 * 0.0625) for r in react2]
 
+    all_of(gather_y, on_y, 0).wait_recv()
+    for j in range(n_y):
+        block[j : j + 1, :] = gather_y[j, 0:1, :]
+    summed = jnp.sum(gather_y[...], axis=0)
+    block[4:7, :] = summed[1:4]
+    block[7:8, :] = summed[0:1]
+    gather[at_z] = block[...]
+    send_all(block, gather.at[at_z], on_z, 1)
+
     for copy in faces:
         copy.wait_recv()
     under = natural([[halo[d, c] for c in range(3)] for d in range(3)], 0)
     source = own_faces - under
     base = join(local_solve(split(source), diag0, scale0, scale1, scale2))
+
+    all_of(gather, on_z, 1).wait_recv()
+    loads[5].wait()
+    rows_y = n_sub // DOM_Z
+    lane_a = iota((rows_y, 128), 1)
+    quads = []
+    for b in range(DOM_Z):
+        places = [(DOM_Z * (a % 2) + b, a // 2) for a in range(rows_y)]
+        quads.append(jnp.concatenate([gather[i, j : j + 1, :] for i, j in places], axis=0))
+
+    def shifted(v, by):
+        return pltpu.roll(v, by % 128, 1) if by % 128 else v
+
+    packed = [
+        jnp.where(lane_a < 96, quads[0], shifted(quads[1], 96)),
+        jnp.where(lane_a < 64, shifted(quads[1], -32), shifted(quads[2], 64)),
+        jnp.where(lane_a < 32, shifted(quads[2], -64), shifted(quads[3], 32)),
+    ]
+    lanes = jnp.zeros((96, 128), F32)
+    for a in range(rows_y):
+        for j in range(3):
+            at = (3 * a + j) * 128
+            lanes = lanes + v_rows[0, :, at : at + 128] * packed[j][a : a + 1, :]
+
+    def lane_total(v):
+        tall = jnp.concatenate([v, jnp.zeros((32, 128), F32)], axis=0)
+        return jnp.sum(jnp.transpose(tall), axis=0, keepdims=True)
+
+    region_row = lane_total(lanes)
+    part = jnp.sum(source * base, axis=0, keepdims=True)
+    part = part[:, :128] + part[:, 128:] + primal_row * region_row
+    packet3[...] = part
+    place = region * n_sub + sub
+    gather3[place] = part
+    send_all(packet3, gather3.at[place], everyone, 3)
+
+    packet2[...] = jnp.sum(gather[...], axis=0)[4:8]
+    gather2[region] = packet2[...]
+    send_all(packet2, gather2.at[region], on_region, 2)
 
     def extract(edge):
         mask_y = tile3(y_lane == edge)
@@ -399,47 +469,10 @@
     for copy in backs:
         copy.start()
 
-    all_of(gather, n_sub, sub_peer, 0).wait_recv()
-    everyone = gather[...]
-    packet2[...] = jnp.sum(everyone, axis=0)
-    gather2[region] = packet2[...]
-    send_all(packet2, gather2.at[region], n_region, region_peer, 1)
-    loads[5].wait()
-    rows_y = n_sub // DOM_Z
-    lane_a = iota((rows_y, 128), 1)
-    quads = []
-    for b in range(DOM_Z):
-        quads.append(jnp.concatenate([gather[DOM_Z * a + b, 0:1, :] for a in range(rows_y)], axis=0))
-
-    def shifted(v, by):
-        return pltpu.roll(v, by % 128, 1) if by % 128 else v
-
-    packed = [
-        jnp.where(lane_a < 96, quads[0], shifted(quads[1], 96)),
-        jnp.where(lane_a < 64, shifted(quads[1], -32), shifted(quads[2], 64)),
-        jnp.where(lane_a < 32, shifted(quads[2], -64), shifted(quads[3], 32)),
-    ]
-    lanes = jnp.zeros((96, 128), F32)
-    for a in range(rows_y):
-        for j in range(3):
-            at = (3 * a + j) * 128
-            lanes = lanes + v_rows[0, :, at : at + 128] * packed[j][a : a + 1, :]
-
-    def lane_total(v):
-        tall = jnp.concatenate([v, jnp.zeros((32, 128), F32)], axis=0)
-        return jnp.sum(jnp.transpose(tall), axis=0, keepdims=True)
-
-    region_row = lane_total(lanes)
-    part = jnp.sum(source * base, axis=0, keepdims=True)
-    part = part[:, :128] + part[:, 128:] + primal_row * region_row
-    packet3[...] = jnp.broadcast_to(part, (8, 128))
-    gather3[sub] = packet3[...]
-    send_all(packet3, gather3.at[sub], n_sub, sub_peer, 2)
-
-    all_of(gather2, n_region, region_peer, 1).wait_recv()
+    all_of(gather2, on_region, 2).wait_recv()
     whole = jnp.sum(gather2[...], axis=0)
-    squares_all = jnp.sum(jnp.where(lane_row == 96, whole[0:1, :], 0.0))
-    total = jnp.concatenate([whole[1:2, :], whole[2:3, :], whole[3:4, :]], axis=1)
+    squares_all = jnp.sum(jnp.where(lane_row == 96, whole[3:4, :], 0.0))
+    total = jnp.concatenate([whole[0:1, :], whole[1:2, :], whole[2:3, :]], axis=1)
     loads[6].wait()
     top = lax.dot_general(
         jnp.broadcast_to(total, (8, 384)),
@@ -466,11 +499,6 @@
     for c in range(3):
         velocity[0, c] = field[CELLS * c : CELLS * c + CELLS]
 
-    all_of(gather3, n_sub, sub_peer, 2).wait_recv()
-    packet4[...] = jnp.sum(gather3[...], axis=0)
-    gather4[region] = packet4[...]
-    send_all(packet4, gather4.at[region], n_region, region_peer, 3)
-
     for copy in backs:
         copy.wait_recv()
     loads[7].wait()
@@ -486,18 +514,16 @@
         for c in range(3):
             jump[d, c] = upper_rows[d][c] + lifted_rows[d][c] - after[d, c]
 
-    all_of(gather4, n_region, region_peer, 3).wait_recv()
-    curvature = jnp.sum(jnp.sum(gather4[...], axis=0)[0:1]) + energy
+    all_of(gather3, everyone, 3).wait_recv()
+    curvature = jnp.sum(gather3[...]) + energy
     alpha[...] = jnp.broadcast_to(squares_all / curvature, (8, 128))
 
-    for copy in faces:
+    for copy in faces + backs:
         copy.wait_send()
-    for copy in backs:
-        copy.wait_send()
-    all_of(gather, n_sub, sub_peer, 0).wait_send()
-    all_of(gather2, n_region, region_peer, 1).wait_send()
-    all_of(gather3, n_sub, sub_peer, 2).wait_send()
-    all_of(gather4, n_region, region_peer, 3).wait_send()
+    all_of(gather_y, on_y, 0).wait_send()
+    all_of(gather, on_z, 1).wait_send()
+    all_of(gather2, on_region, 2).wait_send()
+    all_of(gather3, everyone, 3).wait_send()
 
 
 def finish(multipliers, direction, residual, jump, alpha, velocity, pressure, *outs):
@@ -533,13 +559,13 @@
                 pltpu.VMEM((3, 3, 1, FACE), F32),
                 pltpu.VMEM((3, 3, 1, FACE), F32),
                 pltpu.VMEM((4, 128), F32),
-                pltpu.VMEM((n_sub, 4, 128), F32),
+                pltpu.VMEM((n_sub // Z_LINE, 4, 128), F32),
+                pltpu.VMEM((8, 128), F32),
+                pltpu.VMEM((Z_LINE, 8, 128), F32),
                 pltpu.VMEM((4, 128), F32),
                 pltpu.VMEM((n_region, 4, 128), F32),
-                pltpu.VMEM((8, 128), F32),
-                pltpu.VMEM((n_sub, 8, 128), F32),
-                pltpu.VMEM((8, 128), F32),
-                pltpu.VMEM((n_region, 8, 128), F32),
+                pltpu.VMEM((1, 128), F32),
+                pltpu.VMEM((n_region * n_sub, 1, 128), F32),
                 pltpu.SemaphoreType.DMA((8,)),
                 pltpu.SemaphoreType.DMA((3,)),
                 pltpu.SemaphoreType.DMA((3,)),

time: 32.2 us -> 29.8 us (0.925)
  Pallas kernels: 31.4 us -> 29 us
    pallas_call x1, Pallas kernels: 30.7 us -> 28.3 us  [body(): jump, alpha, velocity, pressure = inner(*args)]
where the time goes in v3:
time: 29.8 us; the launch traced here: 29.7 us
  Pallas kernels  29 us (97%)
  between operations  0.69 us (2%)
    pallas_call x1, Pallas kernels, body(): jump, alpha, velocity, pressure = inner(*args)  28.3 us
    pallas_call x1, Pallas kernels, body(): pl.pallas_call(finish, out_shape=[face, face, cells, scalar_cells], in_sp...  0.71 us

profile of v3, /device:TPU:1, one launch (start us, length us, event | category | flops | bytes accessed | tf_op | source)
XLA Modules:
  0.0 29.7 jit_solution(3471729897780817666)
XLA Ops:
  0.6 0.0 copy-start.1
  0.6 0.0 copy-start
  0.7 0.0 copy-start.2
  0.7 28.3 %feti.1 = (f32[3,3,1,256]{3,2,1,0:T(1,128)S(1)}, f32[8,128]{1,0:T(8,128)S(1)}, f32[1,3,16,256]{3,2,1,0:T(8,128)S(1)}, f32[1,16,256]{2,1,0:T(8,128)S(1)}) custom-call(f32[3,3,1,256]{3,2,1,0:T(1,128)} %bitcast.5, f32[3,3,1,256]{3,2,1,0:T(1,128)} %bitcast.7, f32[1,16,256]{2,1,0:T(8,128)} %reaction.1, f32[1,16,256]{2,1,0:T(8,128)} %viscosity.1, ...), custom_call_target="tpu_custom_call" | custom-call | tf_op jit(solution)/shard_map/feti/pallas_call | solution.py:582
  29.0 0.0 copy-done.1
  29.0 0.0 copy-done
  29.0 0.0 copy-done.2
  29.0 0.7 %finish.1 = (f32[3,3,1,256]{3,2,1,0:T(1,128)}, f32[3,3,1,256]{3,2,1,0:T(1,128)}, f32[1,3,16,256]{3,2,1,0:T(8,128)}, f32[1,16,256]{2,1,0:T(8,128)}) custom-call(f32[3,3,1,256]{3,2,1,0:T(1,128)S(1)} %bitcast.9, f32[3,3,1,256]{3,2,1,0:T(1,128)S(1)} %bitcast.6, f32[3,3,1,256]{3,2,1,0:T(1,128)S(1)} %bitcast.8, f32[3,3,1,256]{3,2,1,0:T(1,128)S(1)} %get-tuple-element.12.jump, ...), custom_call_target="tpu_custom_call" | custom-call | tf_op jit(solution)/shard_map/finish/pallas_call | solution.py:583
Async XLA Ops:
  0.6 28.3 %copy-start.1 = (f32[1,3,3,256]{3,0,2,1:T(1,128)S(1)}, f32[1,3,3,256]{3,0,2,1:T(1,128)}, u32[]{:S(2)}) copy-start(f32[1,3,3,256]{3,0,2,1:T(1,128)} %param.11) | copy-start | bytes 27652
  0.6 28.3 %copy-start = (f32[1,3,3,256]{3,0,2,1:T(1,128)S(1)}, f32[1,3,3,256]{3,0,2,1:T(1,128)}, u32[]{:S(2)}) copy-start(f32[1,3,3,256]{3,0,2,1:T(1,128)} %param.10) | copy-start | bytes 27652
  0.7 28.3 %copy-start.2 = (f32[1,3,3,256]{3,0,2,1:T(1,128)S(1)}, f32[1,3,3,256]{3,0,2,1:T(1,128)}, u32[]{:S(2)}) copy-start(f32[1,3,3,256]{3,0,2,1:T(1,128)} %param.9) | copy-start | bytes 27652

commit v4 on v3

--- a/solution.py
+++ b/solution.py
@@ -20,6 +20,14 @@
 BF16 = jnp.bfloat16
 
 
+def roll(v, by, axis):
+    return pltpu.roll(v, by % v.shape[axis], axis)
+
+
+def flag(condition):
+    return jnp.where(condition, 1.0, 0.0)
+
+
 def iota(shape, axis):
     return lax.broadcasted_iota(jnp.int32, shape, axis)
 
@@ -43,9 +51,6 @@
     lane = iota(shape, 2)
     y = lane >> 4
     z = lane & 15
-
-    def roll(v, by, axis):
-        return pltpu.roll(v, by % v.shape[axis], axis)
 
     sums = []
     ys_up = [roll(v, 16 * step, 2) for v in parts]
@@ -113,27 +118,46 @@
     return [jnp.broadcast_to(v, (3,) + v.shape[1:]) for v in parts]
 
 
-def coarse_solve(source, scale2):
-    b = merge(source)
-    wb = [w * s for w, s in zip(scale2, b)]
+def coarse_weights(scale2):
+    shape = scale2[0].shape
+    x = iota(shape, 1)
+    y = iota(shape, 2) >> 4
+    z = iota(shape, 2) & 15
+    result = []
+    for k, w in enumerate(scale2):
+        near = w * 0.0625
+        other_y = flag(y < 4) if k & 1 else flag(y >= 4)
+        other_x = flag(x < 4) if k & 2 else flag(x >= 4)
+        result.append((near, near * flag(z >= 4), near * flag(z < 12), near * other_y, near * other_x))
+    return result
+
+
+def coarse_solve(source, scale2, weights):
+    wb = [w * s for w, s in zip(scale2, merge(source))]
     v = wb
     for _ in range(COARSE_SWEEPS - 1):
-        near = neighbours(v, 4)
-        v = [KEEP * a + (c + (w * 0.0625) * n) for a, c, w, n in zip(v, wb, scale2, near)]
+        along_y = [roll(a, 64, 2) for a in v]
+        along_x = [roll(a, 4, 1) for a in v]
+        new = []
+        for k, (near, low, high, other_y, other_x) in enumerate(weights):
+            total = (KEEP * v[k] + wb[k]) + near * (along_y[k] + along_x[k])
+            total = total + (other_y * along_y[k ^ 1] + other_x * along_x[k ^ 2])
+            new.append(total + (low * roll(v[k], 4, 2) + high * roll(v[k], -4, 2)))
+        v = new
     return unmerge(v)
 
 
-def middle_solve(source, scale1, scale2):
+def middle_solve(source, scale1, scale2, weights, meanwhile):
     wb = [w * s for w, s in zip(scale1, source)]
     near = neighbours(wb, 2)
     remain = [KEEP * s + 0.25 * n for s, n in zip(source, near)]
-    coarse = coarse_solve(block_mean(remain, 2), scale2)
+    coarse = coarse_solve(block_mean(remain, 2), scale2, weights)
     v = [a + c for a, c in zip(wb, coarse)]
     near = neighbours(v, 2)
     return [KEEP * a + (c + (w * 0.25) * n) for a, c, w, n in zip(v, wb, scale1, near)]
 
 
-def local_solve(source, diag0, scale0, scale1, scale2):
+def local_solve(source, diag0, scale0, scale1, scale2, weights, meanwhile):
     wb = [w * s for w, s in zip(scale0, source)]
     v = None
     for cycle in range(2):
@@ -145,8 +169,10 @@
             v = [KEEP * a + (c + w * n) for a, c, w, n in zip(v, wb, scale0, near)]
             near = neighbours(v, 1)
             remain = [(s - d * a) + n for s, d, a, n in zip(source, diag0, v, near)]
-        coarse = middle_solve(block_mean(remain, 1), scale1, scale2)
+        hook = meanwhile if cycle else lambda: None
+        coarse = middle_solve(block_mean(remain, 1), scale1, scale2, weights, hook)
         v = [a + c for a, c in zip(v, coarse)]
+        hook()
         near = neighbours(v, 1)
         v = [KEEP * a + (c + w * n) for a, c, w, n in zip(v, wb, scale0, near)]
     return v
@@ -162,16 +188,17 @@
 
 
 def spread(rows):
-    own = (iota((CELLS, FACE), 1) >> 4) == iota((CELLS, FACE), 0)
-    return jnp.concatenate([jnp.where(own, jnp.broadcast_to(r, (CELLS, FACE)), 0.0) for r in rows], axis=0)
+    own = (iota((8, 128), 1) >> 4) == iota((8, 128), 0)
+    tiles = [jnp.where(own, jnp.broadcast_to(r[:, h : h + 128], (8, 128)), 0.0) for r in rows for h in (0, 128)]
+    return jnp.concatenate(tiles, axis=0)
 
 
 def collect(field):
-    own = (iota((CELLS, FACE), 1) >> 4) == iota((CELLS, FACE), 0)
-    return [
-        jnp.sum(jnp.where(own, field[CELLS * c : CELLS * c + CELLS], 0.0), axis=0, keepdims=True)
-        for c in range(3)
+    own = (iota((8, 128), 1) >> 4) == iota((8, 128), 0)
+    tiles = [
+        jnp.sum(jnp.where(own, field[8 * i : 8 * i + 8], 0.0), axis=0, keepdims=True) for i in range(6)
     ]
+    return [jnp.concatenate(tiles[2 * c : 2 * c + 2], axis=1) for c in range(3)]
 
 
 def kernel(
@@ -197,19 +224,23 @@
     v_rows,
     v_map,
     v_ginv,
-    table,
+    table_y,
+    table_z,
+    table_back,
     padded_index,
     halo,
     face_send,
     after,
     packet,
     gather_y,
-    block,
     gather,
+    block_sums,
+    gather_sums,
     packet2,
     gather2,
     packet3,
     gather3,
+    sent_rows,
     load_sem,
     halo_send,
     halo_recv,
@@ -222,20 +253,34 @@
     sub = lax.axis_index("sub")
 
     n_y = n_sub // Z_LINE
-    at_y = sub // Z_LINE
-    at_z = lax.rem(sub, Z_LINE)
+    at_y = sub >> (Z_LINE.bit_length() - 1)
+    at_z = sub & (Z_LINE - 1)
 
     def sub_peer(i):
-        return (region, lax.rem(sub + i, n_sub))
+        return (region, (sub + i) & (n_sub - 1))
 
     def region_peer(i):
-        return (lax.rem(region + i, n_region), sub)
+        return ((region + i) & (n_region - 1), sub)
 
     def y_peer(i):
-        return (region, lax.rem(at_y + i, n_y) * Z_LINE + at_z)
+        return (region, ((at_y + i) & (n_y - 1)) * Z_LINE + at_z)
 
     def z_peer(i):
-        return (region, at_y * Z_LINE + lax.rem(at_z + i, Z_LINE))
+        return (region, at_y * Z_LINE + ((at_z + i) & (Z_LINE - 1)))
+
+    barrier = pltpu.get_barrier_semaphore()
+
+    def hops_of(i):
+        carry = [min(j, n_y - j) for j in (i // Z_LINE, (i // Z_LINE + 1) % n_y)]
+        return max(carry) + min(i % Z_LINE, Z_LINE - i % Z_LINE)
+
+    urgent = [n_sub - DOM_Z, n_sub - 1, DOM_Z, 1]
+    others = sorted((i for i in range(1, n_sub) if i not in urgent), key=lambda i: -hops_of(i))
+    near = [sub_peer(i) for i in urgent] + [region_peer(n_region - 1), region_peer(1)]
+    on_sub = [sub_peer(i) for i in others + urgent]
+    near += [sub_peer(i) for i in others] + [region_peer(i) for i in range(2, n_region - 1)]
+    for peer in near:
+        pl.semaphore_signal(barrier, inc=1, device_id=peer, device_id_type=MESH)
 
     loads = [
         pltpu.make_async_copy(src, dst, load_sem.at[i])
@@ -255,14 +300,6 @@
     for load in loads:
         load.start()
 
-    barrier = pltpu.get_barrier_semaphore()
-
-    near = [sub_peer(n_sub - DOM_Z), sub_peer(n_sub - 1), sub_peer(DOM_Z), sub_peer(1)]
-    near += [z_peer(i) for i in range(1, Z_LINE)]
-    near += [y_peer(i) for i in range(1, n_y)] + [region_peer(i) for i in range(1, n_region)]
-    for peer in near:
-        pl.semaphore_signal(barrier, inc=1, device_id=peer, device_id_type=MESH)
-
     def send_all(src, dst_of_me, peers, index):
         for peer in peers:
             pltpu.make_async_remote_copy(
@@ -275,13 +312,13 @@
             ).start()
 
     def all_of(buffer, peers, index):
-        part = buffer.at[pl.ds(0, len(peers))]
+        part = buffer.at[pl.ds(0, len(peers))] if peers else buffer
         return pltpu.make_async_remote_copy(
             src_ref=part,
             dst_ref=part,
             send_sem=sum_send.at[index],
             recv_sem=sum_recv.at[index],
-            device_id=peers[0],
+            device_id=(peers or on_y)[0],
             device_id_type=MESH,
         )
 
@@ -289,8 +326,8 @@
     on_z = [z_peer(i) for i in range(1, Z_LINE)]
     on_region = [region_peer(i) for i in range(1, n_region)]
 
-    at_x = region // 2
-    at_c = lax.rem(region, 2)
+    at_x = region >> 1
+    at_c = region & 1
     n_x = n_region // 2
     found = []
     for dx in range(n_x):
@@ -301,34 +338,13 @@
                         hops = min(dx, n_x - dx) + min(dy, n_y - dy) + min(dz, Z_LINE - dz)
                         found.append((-hops, dx, dc, dy, dz))
     found.sort()
-    xs = [lax.rem(at_x + i, n_x) * 2 for i in range(n_x)]
-    cs = [lax.rem(at_c + i, 2) for i in range(2)]
-    ys = [lax.rem(at_y + i, n_y) * Z_LINE for i in range(n_y)]
-    zs = [lax.rem(at_z + i, Z_LINE) for i in range(Z_LINE)]
+    xs = [((at_x + i) & (n_x - 1)) * 2 for i in range(n_x)]
+    cs = [(at_c + i) & 1 for i in range(2)]
+    ys = [((at_y + i) & (n_y - 1)) * Z_LINE for i in range(n_y)]
+    zs = [((at_z + i) & (Z_LINE - 1)) for i in range(Z_LINE)]
     everyone = [(xs[dx] + cs[dc], ys[dy] + zs[dz]) for _, dx, dc, dy, dz in found]
 
-    row_i = iota((FACE, FACE), 0)
-    col_i = iota((FACE, FACE), 1)
-    table[0] = jnp.where((row_i & 15) == (col_i & 15), 1.0, 0.0).astype(BF16)
-    table[1] = jnp.where((row_i & 15) == (col_i >> 4), 1.0, 0.0).astype(BF16)
-    table[2] = jnp.where((row_i >> 4) == (col_i & 15), 1.0, 0.0).astype(BF16)
-
     loads[0].wait()
-    pl.semaphore_wait(barrier, len(near))
-
-    def face_copy(src, dst, send, recv, peer):
-        return pltpu.make_async_remote_copy(
-            src_ref=src, dst_ref=dst, send_sem=send, recv_sem=recv, device_id=peer, device_id_type=MESH
-        )
-
-    below = (region_peer(n_region - 1), sub_peer(n_sub - DOM_Z), sub_peer(n_sub - 1))
-    faces = [
-        face_copy(v_dir.at[1], halo.at[1], halo_send.at[1], halo_recv.at[1], sub_peer(DOM_Z)),
-        face_copy(v_dir.at[2], halo.at[2], halo_send.at[2], halo_recv.at[2], sub_peer(1)),
-        face_copy(v_dir.at[0], halo.at[0], halo_send.at[0], halo_recv.at[0], region_peer(1)),
-    ]
-    for copy in faces:
-        copy.start()
     loads[1].wait()
     padded_index[...] = jnp.full((8, 128), -1, jnp.int32)
     padded_index[0:1, 0:96] = v_index[...]
@@ -356,25 +372,52 @@
     for j in range(3):
         packet[j + 1 : j + 2, :] = share[:, 128 * j : 128 * j + 128]
     gather_y[at_y] = packet[...]
-
+    gather[sub] = packet[0:1, :]
+
+    pl.semaphore_wait(barrier, len(near))
+
+    def face_copy(src, dst, send, recv, peer):
+        return pltpu.make_async_remote_copy(
+            src_ref=src, dst_ref=dst, send_sem=send, recv_sem=recv, device_id=peer, device_id_type=MESH
+        )
+
+    below = (region_peer(n_region - 1), sub_peer(n_sub - DOM_Z), sub_peer(n_sub - 1))
+    faces = [
+        face_copy(v_dir.at[1], halo.at[1], halo_send.at[1], halo_recv.at[1], sub_peer(DOM_Z)),
+        face_copy(v_dir.at[2], halo.at[2], halo_send.at[2], halo_recv.at[2], sub_peer(1)),
+        face_copy(v_dir.at[0], halo.at[0], halo_send.at[0], halo_recv.at[0], region_peer(1)),
+    ]
+    for copy in faces:
+        copy.start()
+    send_all(packet.at[pl.ds(0, 1)], gather.at[sub], on_sub, 1)
     send_all(packet, gather_y.at[at_y], on_y, 0)
+    row_i = iota((128, FACE), 0)
+    col_i = iota((128, FACE), 1)
+    to_y = jnp.where((row_i[:, :128] & 15) == (col_i[:, :128] & 15), 1.0, 0.0).astype(BF16)
+    to_z = jnp.where((row_i & 15) == (col_i >> 4), 1.0, 0.0).astype(BF16)
+    table_y[...] = to_y
+    table_z[...] = to_z
+    row_i = iota((FACE, 128), 0)
+    col_i = iota((FACE, 128), 1)
+    table_back[...] = jnp.where((row_i >> 4) == (col_i & 15), 1.0, 0.0).astype(BF16)
     lane = iota((CELLS, FACE), 1)
     y_lane = lane >> 4
     z_lane = lane & 15
     x_row = iota((CELLS, FACE), 0)
-    same, to_z, from_z = 0, 1, 2
 
     def tile3(mask):
         return jnp.concatenate([mask] * 3, axis=0)
 
     def natural(face_rows, edge):
-        in_y = exact_dot(spread(face_rows[1]), table[same])
-        in_z = exact_dot(spread(face_rows[2]), table[to_z])
+        in_y = exact_dot(spread(face_rows[1]), table_y[...])
+        in_z = exact_dot(spread(face_rows[2]), table_z[...])
         blocks = []
         for c in range(3):
+            rows = slice(CELLS * c, CELLS * c + CELLS)
+            both = jnp.concatenate([in_y[rows], in_y[rows]], axis=1)
             part = jnp.where(x_row == edge, jnp.broadcast_to(face_rows[0][c], (CELLS, FACE)), 0.0)
-            part = part + jnp.where(y_lane == edge, in_y[CELLS * c : CELLS * c + CELLS], 0.0)
-            part = part + jnp.where(z_lane == edge, in_z[CELLS * c : CELLS * c + CELLS], 0.0)
+            part = part + jnp.where(y_lane == edge, both, 0.0)
+            part = part + jnp.where(z_lane == edge, in_z[rows], 0.0)
             blocks.append(part)
         return jnp.concatenate(blocks, axis=0)
 
@@ -388,66 +431,70 @@
     scale0 = broad([DAMPING / (r + 6.0) for r in react0])
     scale1 = broad([DAMPING / (r + 6.0 * 0.25) for r in react1])
     scale2 = [DAMPING / (r + 6.0 * 0.0625) for r in react2]
+    weights = coarse_weights(scale2)
 
     all_of(gather_y, on_y, 0).wait_recv()
-    for j in range(n_y):
-        block[j : j + 1, :] = gather_y[j, 0:1, :]
     summed = jnp.sum(gather_y[...], axis=0)
-    block[4:7, :] = summed[1:4]
-    block[7:8, :] = summed[0:1]
-    gather[at_z] = block[...]
-    send_all(block, gather.at[at_z], on_z, 1)
+    block_sums[0:3, :] = summed[1:4]
+    block_sums[3:4, :] = summed[0:1]
+    gather_sums[at_z] = block_sums[...]
+    send_all(block_sums, gather_sums.at[at_z], on_z, 4)
+
+    def lane_total(v):
+        tall = jnp.concatenate([v, jnp.zeros((32, 128), F32)], axis=0)
+        return jnp.sum(jnp.transpose(tall), axis=0, keepdims=True)
+
+    region_lanes = []
+
+    def region_operator():
+        all_of(gather, on_sub, 1).wait_recv()
+        loads[5].wait()
+        rows_y = n_sub // DOM_Z
+        lane_a = iota((rows_y, 128), 1)
+        quads = []
+        for b in range(DOM_Z):
+            quads.append(jnp.concatenate([gather[DOM_Z * a + b] for a in range(rows_y)], axis=0))
+
+        def shifted(v, by):
+            return pltpu.roll(v, by % 128, 1) if by % 128 else v
+
+        packed = [
+            jnp.where(lane_a < 96, quads[0], shifted(quads[1], 96)),
+            jnp.where(lane_a < 64, shifted(quads[1], -32), shifted(quads[2], 64)),
+            jnp.where(lane_a < 32, shifted(quads[2], -64), shifted(quads[3], 32)),
+        ]
+        lanes = jnp.zeros((96, 128), F32)
+        for a in range(rows_y):
+            for j in range(3):
+                at = (3 * a + j) * 128
+                lanes = lanes + v_rows[0, :, at : at + 128] * packed[j][a : a + 1, :]
+
+        region_lanes.append(lanes)
 
     for copy in faces:
         copy.wait_recv()
     under = natural([[halo[d, c] for c in range(3)] for d in range(3)], 0)
     source = own_faces - under
-    base = join(local_solve(split(source), diag0, scale0, scale1, scale2))
-
-    all_of(gather, on_z, 1).wait_recv()
-    loads[5].wait()
-    rows_y = n_sub // DOM_Z
-    lane_a = iota((rows_y, 128), 1)
-    quads = []
-    for b in range(DOM_Z):
-        places = [(DOM_Z * (a % 2) + b, a // 2) for a in range(rows_y)]
-        quads.append(jnp.concatenate([gather[i, j : j + 1, :] for i, j in places], axis=0))
-
-    def shifted(v, by):
-        return pltpu.roll(v, by % 128, 1) if by % 128 else v
-
-    packed = [
-        jnp.where(lane_a < 96, quads[0], shifted(quads[1], 96)),
-        jnp.where(lane_a < 64, shifted(quads[1], -32), shifted(quads[2], 64)),
-        jnp.where(lane_a < 32, shifted(quads[2], -64), shifted(quads[3], 32)),
-    ]
-    lanes = jnp.zeros((96, 128), F32)
-    for a in range(rows_y):
-        for j in range(3):
-            at = (3 * a + j) * 128
-            lanes = lanes + v_rows[0, :, at : at + 128] * packed[j][a : a + 1, :]
-
-    def lane_total(v):
-        tall = jnp.concatenate([v, jnp.zeros((32, 128), F32)], axis=0)
-        return jnp.sum(jnp.transpose(tall), axis=0, keepdims=True)
-
-    region_row = lane_total(lanes)
+    base = join(local_solve(split(source), diag0, scale0, scale1, scale2, weights, region_operator))
+
     part = jnp.sum(source * base, axis=0, keepdims=True)
-    part = part[:, :128] + part[:, 128:] + primal_row * region_row
+    part = part[:, :128] + part[:, 128:] + jnp.sum(primal_col * region_lanes[0], axis=0, keepdims=True)
     packet3[...] = part
     place = region * n_sub + sub
-    gather3[place] = part
-    send_all(packet3, gather3.at[place], everyone, 3)
-
-    packet2[...] = jnp.sum(gather[...], axis=0)[4:8]
+    mine = gather3.at[place >> 3, pl.ds(place & 7, 1)]
+    send_all(packet3, mine, everyone, 3)
+    pltpu.make_async_copy(packet3, mine, sum_recv.at[3]).start()
+
+    all_of(gather_sums, on_z, 4).wait_recv()
+    packet2[...] = jnp.sum(gather_sums[...], axis=0)
     gather2[region] = packet2[...]
     send_all(packet2, gather2.at[region], on_region, 2)
 
     def extract(edge):
-        mask_y = tile3(y_lane == edge)
-        mask_z = tile3(z_lane == edge)
-        in_y = collect(exact_dot(jnp.where(mask_y, base, 0.0), table[same]))
-        in_z = collect(exact_dot(jnp.where(mask_z, base, 0.0), table[from_z]))
+        half = 128 if edge else 0
+        at_edge = (iota((3 * CELLS, 128), 1) >> 4) == (edge & 7)
+        in_y = collect(exact_dot(jnp.where(at_edge, base[:, half : half + 128], 0.0), table_y[...]))
+        in_z = collect(exact_dot(jnp.where(tile3(z_lane == edge), base, 0.0), table_back[...]))
         in_x = [base[CELLS * c + edge : CELLS * c + edge + 1] for c in range(3)]
         return [in_x, in_y, in_z]
 
@@ -484,7 +531,7 @@
     energy = jnp.sum(total * top)
     weighted = v_map[0] * top
     lanes = weighted[:, :128] + weighted[:, 128:256] + weighted[:, 256:]
-    lifted = region_row + lane_total(lanes)
+    lifted = lane_total(region_lanes[0] + lanes)
     key_row = jnp.broadcast_to(index_row >> 7, (32, 128))
     placed = jnp.where(key_row == iota((32, 128), 0), jnp.broadcast_to(lifted, (32, 128)), 0.0)
     placed = exact_dot(placed, hit.astype(BF16))
@@ -504,8 +551,9 @@
     loads[7].wait()
     v = [field[CELLS * c : CELLS * c + CELLS] for c in range(3)]
     edge_x = jnp.broadcast_to(after[0, 0], (CELLS, FACE))
-    edge_y = exact_dot(spread([after[1, 1]]), table[same])
-    edge_z = exact_dot(spread([after[2, 2]]), table[to_z])
+    edge_y = exact_dot(spread([after[1, 1]]), table_y[...])
+    edge_y = jnp.concatenate([edge_y, edge_y], axis=1)
+    edge_z = exact_dot(spread([after[2, 2]]), table_z[...])
     step_x = jnp.where(x_row == upper, edge_x, pltpu.roll(v[0], CELLS - 1, 0)) - v[0]
     step_y = jnp.where(y_lane == upper, edge_y, pltpu.roll(v[1], FACE - CELLS, 1)) - v[1]
     step_z = jnp.where(z_lane == upper, edge_z, pltpu.roll(v[2], FACE - 1, 1)) - v[2]
@@ -514,16 +562,17 @@
         for c in range(3):
             jump[d, c] = upper_rows[d][c] + lifted_rows[d][c] - after[d, c]
 
-    all_of(gather3, everyone, 3).wait_recv()
+    all_of(gather3, None, 3).wait_recv()
     curvature = jnp.sum(gather3[...]) + energy
     alpha[...] = jnp.broadcast_to(squares_all / curvature, (8, 128))
 
     for copy in faces + backs:
         copy.wait_send()
     all_of(gather_y, on_y, 0).wait_send()
-    all_of(gather, on_z, 1).wait_send()
+    all_of(gather, on_sub, 1).wait_send()
+    all_of(gather_sums, on_z, 4).wait_send()
     all_of(gather2, on_region, 2).wait_send()
-    all_of(gather3, everyone, 3).wait_send()
+    all_of(sent_rows, None, 3).wait_send()
 
 
 def finish(multipliers, direction, residual, jump, alpha, velocity, pressure, *outs):
@@ -553,26 +602,30 @@
             out_specs=[pl.BlockSpec(memory_space=pltpu.VMEM)] * 4,
             scratch_shapes=[pltpu.VMEM(a.shape, a.dtype) for a in args]
             + [
-                pltpu.VMEM((3, FACE, FACE), BF16),
+                pltpu.VMEM((128, 128), BF16),
+                pltpu.VMEM((128, FACE), BF16),
+                pltpu.VMEM((FACE, 128), BF16),
                 pltpu.VMEM((8, 128), jnp.int32),
                 pltpu.VMEM((3, 3, 1, FACE), F32),
                 pltpu.VMEM((3, 3, 1, FACE), F32),
                 pltpu.VMEM((3, 3, 1, FACE), F32),
                 pltpu.VMEM((4, 128), F32),
                 pltpu.VMEM((n_sub // Z_LINE, 4, 128), F32),
-                pltpu.VMEM((8, 128), F32),
-                pltpu.VMEM((Z_LINE, 8, 128), F32),
+                pltpu.VMEM((n_sub, 1, 128), F32),
+                pltpu.VMEM((4, 128), F32),
+                pltpu.VMEM((Z_LINE, 4, 128), F32),
                 pltpu.VMEM((4, 128), F32),
                 pltpu.VMEM((n_region, 4, 128), F32),
                 pltpu.VMEM((1, 128), F32),
-                pltpu.VMEM((n_region * n_sub, 1, 128), F32),
+                pltpu.VMEM((n_region * n_sub // 8, 8, 128), F32),
+                pltpu.VMEM((n_region * n_sub - 1, 1, 128), F32),
                 pltpu.SemaphoreType.DMA((8,)),
                 pltpu.SemaphoreType.DMA((3,)),
                 pltpu.SemaphoreType.DMA((3,)),
                 pltpu.SemaphoreType.DMA((3,)),
                 pltpu.SemaphoreType.DMA((3,)),
-                pltpu.SemaphoreType.DMA((4,)),
-                pltpu.SemaphoreType.DMA((4,)),
+                pltpu.SemaphoreType.DMA((5,)),
+                pltpu.SemaphoreType.DMA((5,)),
             ],
             compiler_params=pltpu.CompilerParams(
                 collective_id=0, has_side_effects=True, vmem_limit_bytes=VMEM_LIMIT

time: 29.8 us -> 28.4 us (0.953)
  Pallas kernels: 29 us -> 27.6 us
    pallas_call x1, Pallas kernels: 28.3 us -> 26.9 us  [body(): jump, alpha, velocity, pressure = inner(*args)]
where the time goes in v4:
time: 28.4 us; the launch traced here: 28.3 us
  Pallas kernels  27.6 us (97%)
  between operations  0.69 us (2%)
    pallas_call x1, Pallas kernels, body(): jump, alpha, velocity, pressure = inner(*args)  26.9 us
    pallas_call x1, Pallas kernels, body(): pl.pallas_call(finish, out_shape=[face, face, cells, scalar_cells], in_sp...  0.71 us

profile of v4, /device:TPU:1, one launch (start us, length us, event | category | flops | bytes accessed | tf_op | source)
XLA Modules:
  0.0 28.3 jit_solution(3425687096276570812)
XLA Ops:
  0.6 0.0 copy-start.1
  0.6 0.0 copy-start
  0.7 0.0 copy-start.2
  0.7 26.9 %feti.1 = (f32[3,3,1,256]{3,2,1,0:T(1,128)S(1)}, f32[8,128]{1,0:T(8,128)S(1)}, f32[1,3,16,256]{3,2,1,0:T(8,128)S(1)}, f32[1,16,256]{2,1,0:T(8,128)S(1)}) custom-call(f32[3,3,1,256]{3,2,1,0:T(1,128)} %bitcast.5, f32[3,3,1,256]{3,2,1,0:T(1,128)} %bitcast.7, f32[1,16,256]{2,1,0:T(8,128)} %reaction.1, f32[1,16,256]{2,1,0:T(8,128)} %viscosity.1, ...), custom_call_target="tpu_custom_call" | custom-call | tf_op jit(solution)/shard_map/feti/pallas_call | solution.py:635
  27.6 0.0 copy-done.1
  27.6 0.0 copy-done
  27.6 0.0 copy-done.2
  27.6 0.7 %finish.1 = (f32[3,3,1,256]{3,2,1,0:T(1,128)}, f32[3,3,1,256]{3,2,1,0:T(1,128)}, f32[1,3,16,256]{3,2,1,0:T(8,128)}, f32[1,16,256]{2,1,0:T(8,128)}) custom-call(f32[3,3,1,256]{3,2,1,0:T(1,128)S(1)} %bitcast.9, f32[3,3,1,256]{3,2,1,0:T(1,128)S(1)} %bitcast.6, f32[3,3,1,256]{3,2,1,0:T(1,128)S(1)} %bitcast.8, f32[3,3,1,256]{3,2,1,0:T(1,128)S(1)} %get-tuple-element.12.jump, ...), custom_call_target="tpu_custom_call" | custom-call | tf_op jit(solution)/shard_map/finish/pallas_call | solution.py:636
Async XLA Ops:
  0.6 27.0 %copy-start.1 = (f32[1,3,3,256]{3,0,2,1:T(1,128)S(1)}, f32[1,3,3,256]{3,0,2,1:T(1,128)}, u32[]{:S(2)}) copy-start(f32[1,3,3,256]{3,0,2,1:T(1,128)} %param.11) | copy-start | bytes 27652
  0.6 27.0 %copy-start = (f32[1,3,3,256]{3,0,2,1:T(1,128)S(1)}, f32[1,3,3,256]{3,0,2,1:T(1,128)}, u32[]{:S(2)}) copy-start(f32[1,3,3,256]{3,0,2,1:T(1,128)} %param.10) | copy-start | bytes 27652
  0.7 27.0 %copy-start.2 = (f32[1,3,3,256]{3,0,2,1:T(1,128)S(1)}, f32[1,3,3,256]{3,0,2,1:T(1,128)}, u32[]{:S(2)}) copy-start(f32[1,3,3,256]{3,0,2,1:T(1,128)} %param.9) | copy-start | bytes 27652

commit v5 on v4

--- a/solution.py
+++ b/solution.py
@@ -93,23 +93,35 @@
     return result
 
 
-def merge(parts):
-    spot = iota(parts[0].shape[1:], 1) & 3
-    return [jnp.where(spot == 0, v[0], jnp.where(spot == 1, v[1], v[2]))[None] for v in parts]
+def merge_mean(parts):
+    lane = iota((8, 128), 1)
+    odd_z, odd_y = (lane & 1) == 1, ((lane >> 4) & 1) == 1
+    even_x = (iota((8, 128), 0) & 1) == 0
+    result = []
+    for v in parts:
+        a = v[0] + roll(v[0], -1, 1)
+        b = v[1] + roll(v[1], 1, 1)
+        c = v[2] + roll(v[2], -1, 1)
+        a, b, c = a + roll(a, -16, 1), b + roll(b, -16, 1), c + roll(c, 16, 1)
+        m = jnp.where(odd_y, c, jnp.where(odd_z, b, a))
+        m = m + jnp.where(even_x, roll(m, -1, 0), roll(m, 1, 0))
+        result.append((m * 0.125)[None])
+    return result
 
 
 def unmerge(parts):
+    lane = iota((8, 128), 1)
+    odd_z, odd_y = (lane & 1) == 1, ((lane >> 4) & 1) == 1
     result = []
     for v in parts:
         v = v[0]
-        spot = iota(v.shape, 1) & 3
-        moved = {by: pltpu.roll(v, by % 128, 1) if by else v for by in range(-2, 4)}
-        comps = []
-        for c in range(3):
-            value = moved[3 - c]
-            for t in (2, 1, 0):
-                value = jnp.where(spot == t, moved[t - c], value)
-            comps.append(value)
+        even = jnp.where(odd_z, roll(v, 1, 1), v)
+        odd = jnp.where(odd_z, v, roll(v, -1, 1))
+        comps = [
+            jnp.where(odd_y, roll(even, 16, 1), even),
+            jnp.where(odd_y, roll(odd, 16, 1), odd),
+            jnp.where(odd_y, even, roll(even, -16, 1)),
+        ]
         result.append(jnp.stack(comps, axis=0))
     return result
 
@@ -133,7 +145,7 @@
 
 
 def coarse_solve(source, scale2, weights):
-    wb = [w * s for w, s in zip(scale2, merge(source))]
+    wb = [w * s for w, s in zip(scale2, source)]
     v = wb
     for _ in range(COARSE_SWEEPS - 1):
         along_y = [roll(a, 64, 2) for a in v]
@@ -144,7 +156,7 @@
             total = total + (other_y * along_y[k ^ 1] + other_x * along_x[k ^ 2])
             new.append(total + (low * roll(v[k], 4, 2) + high * roll(v[k], -4, 2)))
         v = new
-    return unmerge(v)
+    return v
 
 
 def middle_solve(source, scale1, scale2, weights, meanwhile):
@@ -154,7 +166,7 @@
     coarse = coarse_solve(block_mean(remain, 2), scale2, weights)
     v = [a + c for a, c in zip(wb, coarse)]
     near = neighbours(v, 2)
-    return [KEEP * a + (c + (w * 0.25) * n) for a, c, w, n in zip(v, wb, scale1, near)]
+    return unmerge([KEEP * a + (c + (w * 0.25) * n) for a, c, w, n in zip(v, wb, scale1, near)])
 
 
 def local_solve(source, diag0, scale0, scale1, scale2, weights, meanwhile):
@@ -170,7 +182,7 @@
             near = neighbours(v, 1)
             remain = [(s - d * a) + n for s, d, a, n in zip(source, diag0, v, near)]
         hook = meanwhile if cycle else lambda: None
-        coarse = middle_solve(block_mean(remain, 1), scale1, scale2, weights, hook)
+        coarse = middle_solve(merge_mean(remain), scale1, scale2, weights, hook)
         v = [a + c for a, c in zip(v, coarse)]
         hook()
         near = neighbours(v, 1)
@@ -183,8 +195,9 @@
     rest = left - high.astype(F32)
     mid = rest.astype(BF16)
     low = (rest - mid.astype(F32)).astype(BF16)
-    dot = functools.partial(jnp.dot, preferred_element_type=F32)
-    return dot(high, right) + (dot(mid, right) + dot(low, right))
+    whole = jnp.dot(jnp.concatenate([high, mid, low], axis=0), right, preferred_element_type=F32)
+    n = left.shape[0]
+    return whole[:n] + (whole[n : 2 * n] + whole[2 * n :])
 
 
 def spread(rows):
@@ -268,20 +281,6 @@
     def z_peer(i):
         return (region, at_y * Z_LINE + ((at_z + i) & (Z_LINE - 1)))
 
-    barrier = pltpu.get_barrier_semaphore()
-
-    def hops_of(i):
-        carry = [min(j, n_y - j) for j in (i // Z_LINE, (i // Z_LINE + 1) % n_y)]
-        return max(carry) + min(i % Z_LINE, Z_LINE - i % Z_LINE)
-
-    urgent = [n_sub - DOM_Z, n_sub - 1, DOM_Z, 1]
-    others = sorted((i for i in range(1, n_sub) if i not in urgent), key=lambda i: -hops_of(i))
-    near = [sub_peer(i) for i in urgent] + [region_peer(n_region - 1), region_peer(1)]
-    on_sub = [sub_peer(i) for i in others + urgent]
-    near += [sub_peer(i) for i in others] + [region_peer(i) for i in range(2, n_region - 1)]
-    for peer in near:
-        pl.semaphore_signal(barrier, inc=1, device_id=peer, device_id_type=MESH)
-
     loads = [
         pltpu.make_async_copy(src, dst, load_sem.at[i])
         for i, (src, dst) in enumerate(
@@ -299,6 +298,20 @@
     ]
     for load in loads:
         load.start()
+
+    barrier = pltpu.get_barrier_semaphore()
+
+    def hops_of(i):
+        carry = [min(j, n_y - j) for j in (i // Z_LINE, (i // Z_LINE + 1) % n_y)]
+        return max(carry) + min(i % Z_LINE, Z_LINE - i % Z_LINE)
+
+    urgent = [n_sub - DOM_Z, n_sub - 1, DOM_Z, 1]
+    others = sorted((i for i in range(1, n_sub) if i not in urgent), key=lambda i: -hops_of(i))
+    near = [sub_peer(i) for i in urgent] + [region_peer(n_region - 1), region_peer(1)]
+    on_sub = [sub_peer(i) for i in others + urgent]
+    near += [sub_peer(i) for i in others] + [region_peer(i) for i in range(2, n_region - 1)]
+    for peer in near:
+        pl.semaphore_signal(barrier, inc=1, device_id=peer, device_id_type=MESH)
 
     def send_all(src, dst_of_me, peers, index):
         for peer in peers:
@@ -383,8 +396,8 @@
 
     below = (region_peer(n_region - 1), sub_peer(n_sub - DOM_Z), sub_peer(n_sub - 1))
     faces = [
-        face_copy(v_dir.at[1], halo.at[1], halo_send.at[1], halo_recv.at[1], sub_peer(DOM_Z)),
-        face_copy(v_dir.at[2], halo.at[2], halo_send.at[2], halo_recv.at[2], sub_peer(1)),
+        face_copy(v_dir.at[1], halo.at[1], halo_send.at[0], halo_recv.at[0], sub_peer(DOM_Z)),
+        face_copy(v_dir.at[2], halo.at[2], halo_send.at[0], halo_recv.at[0], sub_peer(1)),
         face_copy(v_dir.at[0], halo.at[0], halo_send.at[0], halo_recv.at[0], region_peer(1)),
     ]
     for copy in faces:
@@ -429,7 +442,7 @@
     react2 = block_mean(react1, 2)
     diag0 = broad([r + 6.0 for r in react0])
     scale0 = broad([DAMPING / (r + 6.0) for r in react0])
-    scale1 = broad([DAMPING / (r + 6.0 * 0.25) for r in react1])
+    scale1 = [DAMPING / (r + 6.0 * 0.25) for r in react1]
     scale2 = [DAMPING / (r + 6.0 * 0.0625) for r in react2]
     weights = coarse_weights(scale2)
 
@@ -471,8 +484,8 @@
 
         region_lanes.append(lanes)
 
-    for copy in faces:
-        copy.wait_recv()
+    all_faces = face_copy(halo, halo, halo_send.at[0], halo_recv.at[0], sub_peer(1))
+    all_faces.wait_recv()
     under = natural([[halo[d, c] for c in range(3)] for d in range(3)], 0)
     source = own_faces - under
     base = join(local_solve(split(source), diag0, scale0, scale1, scale2, weights, region_operator))
@@ -482,13 +495,8 @@
     packet3[...] = part
     place = region * n_sub + sub
     mine = gather3.at[place >> 3, pl.ds(place & 7, 1)]
-    send_all(packet3, mine, everyone, 3)
+    send_all(packet3, mine, everyone[:46], 3)
     pltpu.make_async_copy(packet3, mine, sum_recv.at[3]).start()
-
-    all_of(gather_sums, on_z, 4).wait_recv()
-    packet2[...] = jnp.sum(gather_sums[...], axis=0)
-    gather2[region] = packet2[...]
-    send_all(packet2, gather2.at[region], on_region, 2)
 
     def extract(edge):
         half = 128 if edge else 0
@@ -506,8 +514,8 @@
         pltpu.make_async_remote_copy(
             src_ref=face_send.at[d],
             dst_ref=after.at[d],
-            send_sem=back_send.at[d],
-            recv_sem=back_recv.at[d],
+            send_sem=back_send.at[0],
+            recv_sem=back_recv.at[0],
             device_id=below[d],
             device_id_type=MESH,
         )
@@ -515,6 +523,15 @@
     ]
     for copy in backs:
         copy.start()
+
+    send_all(packet3, mine, everyone[46:158], 3)
+
+    all_of(gather_sums, on_z, 4).wait_recv()
+    packet2[...] = jnp.sum(gather_sums[...], axis=0)
+    gather2[region] = packet2[...]
+    send_all(packet2, gather2.at[region], on_region, 2)
+
+    send_all(packet3, mine, everyone[158:], 3)
 
     all_of(gather2, on_region, 2).wait_recv()
     whole = jnp.sum(gather2[...], axis=0)
@@ -546,8 +563,8 @@
     for c in range(3):
         velocity[0, c] = field[CELLS * c : CELLS * c + CELLS]
 
-    for copy in backs:
-        copy.wait_recv()
+    all_backs = face_copy(after, after, back_send.at[0], back_recv.at[0], sub_peer(1))
+    all_backs.wait_recv()
     loads[7].wait()
     v = [field[CELLS * c : CELLS * c + CELLS] for c in range(3)]
     edge_x = jnp.broadcast_to(after[0, 0], (CELLS, FACE))
@@ -566,8 +583,8 @@
     curvature = jnp.sum(gather3[...]) + energy
     alpha[...] = jnp.broadcast_to(squares_all / curvature, (8, 128))
 
-    for copy in faces + backs:
-        copy.wait_send()
+    all_faces.wait_send()
+    all_backs.wait_send()
     all_of(gather_y, on_y, 0).wait_send()
     all_of(gather, on_sub, 1).wait_send()
     all_of(gather_sums, on_z, 4).wait_send()
@@ -620,10 +637,10 @@
                 pltpu.VMEM((n_region * n_sub // 8, 8, 128), F32),
                 pltpu.VMEM((n_region * n_sub - 1, 1, 128), F32),
                 pltpu.SemaphoreType.DMA((8,)),
-                pltpu.SemaphoreType.DMA((3,)),
-                pltpu.SemaphoreType.DMA((3,)),
-                pltpu.SemaphoreType.DMA((3,)),
-                pltpu.SemaphoreType.DMA((3,)),
+                pltpu.SemaphoreType.DMA((1,)),
+                pltpu.SemaphoreType.DMA((1,)),
+                pltpu.SemaphoreType.DMA((1,)),
+                pltpu.SemaphoreType.DMA((1,)),
                 pltpu.SemaphoreType.DMA((5,)),
                 pltpu.SemaphoreType.DMA((5,)),
             ],

time: 28.4 us -> 28.2 us (level)
  no operation moved by 1% of the time
where the time goes in v5:
time: 28.2 us; the launch traced here: 28.1 us
  Pallas kernels  27.4 us (97%)
  between operations  0.69 us (2%)
    pallas_call x1, Pallas kernels, body(): jump, alpha, velocity, pressure = inner(*args)  26.7 us
    pallas_call x1, Pallas kernels, body(): pl.pallas_call(finish, out_shape=[face, face, cells, scalar_cells], in_sp...  0.71 us

profile of v5, /device:TPU:1, one launch (start us, length us, event | category | flops | bytes accessed | tf_op | source)
XLA Modules:
  0.0 28.1 jit_solution(17847085408675273945)
XLA Ops:
  0.6 0.0 copy-start.1
  0.6 0.0 copy-start
  0.7 0.0 copy-start.2
  0.7 26.7 %feti.1 = (f32[3,3,1,256]{3,2,1,0:T(1,128)S(1)}, f32[8,128]{1,0:T(8,128)S(1)}, f32[1,3,16,256]{3,2,1,0:T(8,128)S(1)}, f32[1,16,256]{2,1,0:T(8,128)S(1)}) custom-call(f32[3,3,1,256]{3,2,1,0:T(1,128)} %bitcast.5, f32[3,3,1,256]{3,2,1,0:T(1,128)} %bitcast.7, f32[1,16,256]{2,1,0:T(8,128)} %reaction.1, f32[1,16,256]{2,1,0:T(8,128)} %viscosity.1, ...), custom_call_target="tpu_custom_call" | custom-call | tf_op jit(solution)/shard_map/feti/pallas_call | solution.py:652
  27.4 0.0 copy-done.1
  27.4 0.0 copy-done
  27.4 0.0 copy-done.2
  27.4 0.7 %finish.1 = (f32[3,3,1,256]{3,2,1,0:T(1,128)}, f32[3,3,1,256]{3,2,1,0:T(1,128)}, f32[1,3,16,256]{3,2,1,0:T(8,128)}, f32[1,16,256]{2,1,0:T(8,128)}) custom-call(f32[3,3,1,256]{3,2,1,0:T(1,128)S(1)} %bitcast.9, f32[3,3,1,256]{3,2,1,0:T(1,128)S(1)} %bitcast.6, f32[3,3,1,256]{3,2,1,0:T(1,128)S(1)} %bitcast.8, f32[3,3,1,256]{3,2,1,0:T(1,128)S(1)} %get-tuple-element.12.jump, ...), custom_call_target="tpu_custom_call" | custom-call | tf_op jit(solution)/shard_map/finish/pallas_call | solution.py:653
Async XLA Ops:
  0.6 26.7 %copy-start.1 = (f32[1,3,3,256]{3,0,2,1:T(1,128)S(1)}, f32[1,3,3,256]{3,0,2,1:T(1,128)}, u32[]{:S(2)}) copy-start(f32[1,3,3,256]{3,0,2,1:T(1,128)} %param.11) | copy-start | bytes 27652
  0.6 26.7 %copy-start = (f32[1,3,3,256]{3,0,2,1:T(1,128)S(1)}, f32[1,3,3,256]{3,0,2,1:T(1,128)}, u32[]{:S(2)}) copy-start(f32[1,3,3,256]{3,0,2,1:T(1,128)} %param.10) | copy-start | bytes 27652
  0.7 26.7 %copy-start.2 = (f32[1,3,3,256]{3,0,2,1:T(1,128)S(1)}, f32[1,3,3,256]{3,0,2,1:T(1,128)}, u32[]{:S(2)}) copy-start(f32[1,3,3,256]{3,0,2,1:T(1,128)} %param.9) | copy-start | bytes 27652

commit v6 on v5

--- a/solution.py
+++ b/solution.py
@@ -296,7 +296,7 @@
             )
         )
     ]
-    for load in loads:
+    for load in loads[:3]:
         load.start()
 
     barrier = pltpu.get_barrier_semaphore()
@@ -307,11 +307,15 @@
 
     urgent = [n_sub - DOM_Z, n_sub - 1, DOM_Z, 1]
     others = sorted((i for i in range(1, n_sub) if i not in urgent), key=lambda i: -hops_of(i))
-    near = [sub_peer(i) for i in urgent] + [region_peer(n_region - 1), region_peer(1)]
+    near = [sub_peer(i) for i in others[:2]] + [sub_peer(i) for i in urgent]
+    near += [region_peer(n_region - 1), region_peer(1)]
     on_sub = [sub_peer(i) for i in others + urgent]
-    near += [sub_peer(i) for i in others] + [region_peer(i) for i in range(2, n_region - 1)]
+    near += [sub_peer(i) for i in others[2:]] + [region_peer(i) for i in range(2, n_region - 1)]
     for peer in near:
         pl.semaphore_signal(barrier, inc=1, device_id=peer, device_id_type=MESH)
+
+    for load in loads[3:]:
+        load.start()
 
     def send_all(src, dst_of_me, peers, index):
         for peer in peers:
@@ -358,6 +362,21 @@
     everyone = [(xs[dx] + cs[dc], ys[dy] + zs[dz]) for _, dx, dc, dy, dz in found]
 
     loads[0].wait()
+    pl.semaphore_wait(barrier, len(near))
+
+    def face_copy(src, dst, send, recv, peer):
+        return pltpu.make_async_remote_copy(
+            src_ref=src, dst_ref=dst, send_sem=send, recv_sem=recv, device_id=peer, device_id_type=MESH
+        )
+
+    below = (region_peer(n_region - 1), sub_peer(n_sub - DOM_Z), sub_peer(n_sub - 1))
+    faces = [
+        face_copy(v_dir.at[1], halo.at[1], halo_send.at[0], halo_recv.at[0], sub_peer(DOM_Z)),
+        face_copy(v_dir.at[2], halo.at[2], halo_send.at[0], halo_recv.at[0], sub_peer(1)),
+        face_copy(v_dir.at[0], halo.at[0], halo_send.at[0], halo_recv.at[0], region_peer(1)),
+    ]
+    for copy in faces:
+        copy.start()
     loads[1].wait()
     padded_index[...] = jnp.full((8, 128), -1, jnp.int32)
     padded_index[0:1, 0:96] = v_index[...]
@@ -387,21 +406,6 @@
     gather_y[at_y] = packet[...]
     gather[sub] = packet[0:1, :]
 
-    pl.semaphore_wait(barrier, len(near))
-
-    def face_copy(src, dst, send, recv, peer):
-        return pltpu.make_async_remote_copy(
-            src_ref=src, dst_ref=dst, send_sem=send, recv_sem=recv, device_id=peer, device_id_type=MESH
-        )
-
-    below = (region_peer(n_region - 1), sub_peer(n_sub - DOM_Z), sub_peer(n_sub - 1))
-    faces = [
-        face_copy(v_dir.at[1], halo.at[1], halo_send.at[0], halo_recv.at[0], sub_peer(DOM_Z)),
-        face_copy(v_dir.at[2], halo.at[2], halo_send.at[0], halo_recv.at[0], sub_peer(1)),
-        face_copy(v_dir.at[0], halo.at[0], halo_send.at[0], halo_recv.at[0], region_peer(1)),
-    ]
-    for copy in faces:
-        copy.start()
     send_all(packet.at[pl.ds(0, 1)], gather.at[sub], on_sub, 1)
     send_all(packet, gather_y.at[at_y], on_y, 0)
     row_i = iota((128, FACE), 0)

time: 28.2 us -> 28.1 us (level)
  no operation moved by 1% of the time
where the time goes in v6:
time: 28.1 us; the launch traced here: 28 us
  Pallas kernels  27.3 us (97%)
  between operations  0.69 us (2%)
    pallas_call x1, Pallas kernels, body(): jump, alpha, velocity, pressure = inner(*args)  26.6 us
    pallas_call x1, Pallas kernels, body(): pl.pallas_call(finish, out_shape=[face, face, cells, scalar_cells], in_sp...  0.71 us

profile of v6, /device:TPU:1, one launch (start us, length us, event | category | flops | bytes accessed | tf_op | source)
XLA Modules:
  0.0 28.0 jit_solution(17708481918706303015)
XLA Ops:
  0.6 0.0 copy-start.1
  0.6 0.0 copy-start
  0.7 0.0 copy-start.2
  0.7 26.6 %feti.1 = (f32[3,3,1,256]{3,2,1,0:T(1,128)S(1)}, f32[8,128]{1,0:T(8,128)S(1)}, f32[1,3,16,256]{3,2,1,0:T(8,128)S(1)}, f32[1,16,256]{2,1,0:T(8,128)S(1)}) custom-call(f32[3,3,1,256]{3,2,1,0:T(1,128)} %bitcast.5, f32[3,3,1,256]{3,2,1,0:T(1,128)} %bitcast.7, f32[1,16,256]{2,1,0:T(8,128)} %reaction.1, f32[1,16,256]{2,1,0:T(8,128)} %viscosity.1, ...), custom_call_target="tpu_custom_call" | custom-call | tf_op jit(solution)/shard_map/feti/pallas_call | solution.py:656
  27.3 0.0 copy-done.1
  27.3 0.0 copy-done
  27.3 0.0 copy-done.2
  27.3 0.7 %finish.1 = (f32[3,3,1,256]{3,2,1,0:T(1,128)}, f32[3,3,1,256]{3,2,1,0:T(1,128)}, f32[1,3,16,256]{3,2,1,0:T(8,128)}, f32[1,16,256]{2,1,0:T(8,128)}) custom-call(f32[3,3,1,256]{3,2,1,0:T(1,128)S(1)} %bitcast.9, f32[3,3,1,256]{3,2,1,0:T(1,128)S(1)} %bitcast.6, f32[3,3,1,256]{3,2,1,0:T(1,128)S(1)} %bitcast.8, f32[3,3,1,256]{3,2,1,0:T(1,128)S(1)} %get-tuple-element.12.jump, ...), custom_call_target="tpu_custom_call" | custom-call | tf_op jit(solution)/shard_map/finish/pallas_call | solution.py:657
Async XLA Ops:
  0.6 26.7 %copy-start.1 = (f32[1,3,3,256]{3,0,2,1:T(1,128)S(1)}, f32[1,3,3,256]{3,0,2,1:T(1,128)}, u32[]{:S(2)}) copy-start(f32[1,3,3,256]{3,0,2,1:T(1,128)} %param.11) | copy-start | bytes 27652
  0.6 26.7 %copy-start = (f32[1,3,3,256]{3,0,2,1:T(1,128)S(1)}, f32[1,3,3,256]{3,0,2,1:T(1,128)}, u32[]{:S(2)}) copy-start(f32[1,3,3,256]{3,0,2,1:T(1,128)} %param.10) | copy-start | bytes 27652
  0.7 26.7 %copy-start.2 = (f32[1,3,3,256]{3,0,2,1:T(1,128)S(1)}, f32[1,3,3,256]{3,0,2,1:T(1,128)}, u32[]{:S(2)}) copy-start(f32[1,3,3,256]{3,0,2,1:T(1,128)} %param.9) | copy-start | bytes 27652
